TPU v7x, 32 devices: a whole 2x2x4 slice. The times are simulated.
32 devices in a mesh: bx: 8 (over z, y), by: 4 (over x, core).
Axes of the slice: x: 2, y: 2, z: 4, core: 2. Of those that a mesh axis runs over, the one named last changes fastest.
Arguments:
- polarization: float32 [3, 8, 256, 512], P(None, None, 'bx', 'by'), may hold values from -1.6 to 1.6
- alpha_field: float32 [8, 256, 512], P(None, 'bx', 'by'), may hold values from -1 to 1
- landau: float32 [3, 8], replicated, may hold values from 0.05 to 0.25
- stiffness: float32 [8], replicated, may hold values from 0.5 to 1.5
- permittivity: float32 [8], replicated, may hold values from 0.5 to 2
- interfaces: float32 [9], replicated, may hold values from 0.0002 to 0.0008
Outputs:
- polar_next: float32 [3, 8, 256, 512], P(None, None, 'bx', 'by')
- depol_field: float32 [3, 8, 256, 512], P(None, None, 'bx', 'by')
All inputs are finite; a program needn't handle non-finite values.
Results may differ from a plain program's by a relative error of at most 0.0003.
Values sent between devices are 32-bit elements; how exact they have to be, the bound alone decides.
A program may use at most 64 MiB of HBM per device.

v0:
```python
import functools

import jax
import jax.numpy as jnp
import numpy as np
from jax import lax
from jax.experimental import pallas as pl
from jax.experimental.pallas import tpu as pltpu
from jax.sharding import PartitionSpec as P

STEPS = 2
step_size = 0.05
MESH = pl.DeviceIdType.MESH
PAD = 8


def cas_table(left, right, length):
    turns = left * right % length
    angle = 2.0 * jnp.pi / length * turns.astype(jnp.float32)
    table = jnp.cos(angle) + jnp.sin(angle)
    high = lax.reduce_precision(table, 8, 7)
    return jnp.stack([high.astype(jnp.bfloat16), (table - high).astype(jnp.bfloat16)])


def fixed_table(left, right, length):
    angle = 2.0 * np.pi / length * (left * right % length)
    table = (np.cos(angle) + np.sin(angle)).astype(np.float32)
    high = table.astype(jnp.bfloat16)
    low = (table - high.astype(np.float32)).astype(jnp.bfloat16)
    return jnp.asarray(np.stack([high, low]))


def is_wide(rows, nbx, nby, layers):
    return layers % nbx == 0 and rows % (8 * nby) == 0


def halves(value):
    high = value.astype(jnp.bfloat16)
    low = (value - high.astype(jnp.float32)).astype(jnp.bfloat16)
    return high, low


def product(left, right):
    dot = functools.partial(jnp.dot, preferred_element_type=jnp.float32)
    return dot(left[0], right[0]) + (dot(left[0], right[1]) + dot(left[1], right[0]))


def kernel(sizes, p_in, alpha_h, landau, stiff, perm, inter, lam, hx_h, hy_h, p_out, f_out, *scratch):
    L, R, C, nbx, nby, rep, lp, own = sizes
    (p_mid, base, coef, ratio, q, inb, outs, rec_i,
     row_s, row_r, col_s, col_r, pc_s, pc_r, ssem, rsem,
     alpha, hx, hy, local_sem) = scratch[:20]
    wide = is_wide(R, nbx, nby, L)
    if wide:
        z_in, w_out = scratch[20:]
    else:
        rec_f, ybuf, phat, u = scratch[20:]
    thin = R // nby
    R2 = R + PAD
    bx = lax.axis_index("bx")
    by = lax.axis_index("by")
    group = bx // rep
    part = bx % rep
    scale = 1.0 / (R * nbx * C * nby)
    loads = [pltpu.make_async_copy(src, dst, local_sem.at[at]) for at, (src, dst) in
             enumerate(((alpha_h, alpha), (hx_h, hx), (hy_h, hy)))]
    for load in loads:
        load.start()
    slots = [0]
    sends = []

    barrier = pltpu.get_barrier_semaphore()
    others = [(a, b) for b in range(nby) for a in range(nbx) if a or b]
    greeted = [(a, b) for a, b in others if wide or not a or not b]
    for a, b in greeted:
        pl.semaphore_signal(
            barrier, inc=1, device_id={"bx": (bx + a) % nbx, "by": (by + b) % nby},
            device_id_type=MESH)

    def remote(src, dst, device, slot):
        return pltpu.make_async_remote_copy(
            src_ref=src, dst_ref=dst, send_sem=ssem.at[slot], recv_sem=rsem.at[slot],
            device_id=device, device_id_type=MESH)

    def fresh():
        slots[0] += 1
        return slots[0] - 1

    def push(src, dst, device):
        copy = remote(src, dst, device, fresh())
        copy.start()
        sends.append(copy.wait_send)
        return copy

    rows = lax.broadcasted_iota(jnp.int32, (R, C), 0)
    lanes = lax.broadcasted_iota(jnp.int32, (R, C), 1)

    def x_next(f, high):
        return jnp.where(rows == R - 1, high, pltpu.roll(f, R - 1, 0))

    def x_prev(f, low):
        return jnp.where(rows == 0, low, pltpu.roll(f, 1, 0))

    def y_next(f, high):
        return jnp.where(lanes == C - 1, high, pltpu.roll(f, C - 1, 1))

    def y_prev(f, low):
        return jnp.where(lanes == 0, low, pltpu.roll(f, 1, 1))

    def column_tile(blocks):
        tile = jnp.zeros((R, C), jnp.float32)
        for at, block in enumerate(blocks):
            tile = jnp.where(lanes == at, block[:, 0:1], tile)
            tile = jnp.where(lanes == C // 2 + at, block[:, C - 1:C], tile)
        return tile

    def x_start(src, n):
        mine = inb.at[n, :, pl.ds(pl.multiple_of(bx * R, R), R)]
        copies = []
        for k in range(1, nbx):
            to = (bx + k) % nbx
            copies.append(push(src.at[pl.ds(to // rep * lp, lp)], mine, {"bx": to}))
        for layer in range(lp):
            inb[n, layer, pl.ds(pl.multiple_of(bx * R, R), R)] = src[group * lp + layer]
        return copies

    def x_mix(copies, n):
        for copy in copies:
            copy.wait_recv()
        table = (hx[0], hx[1])
        for layer in range(lp):
            outs[n, :, layer] = product(table, halves(inb[n, layer])).reshape(own, R2, C)

    def spread(n, step):
        copies = []
        for a, b in others:
            to_x, to_y = (bx + a) % nbx, (by + b) % nby
            copies.append(push(
                outs.at[n, to_x, :, pl.ds(pl.multiple_of(to_y * thin, thin), thin)],
                z_in.at[step, by, pl.ds(bx * lp, lp)], {"bx": to_x, "by": to_y}))
        for layer in range(lp):
            z_in[step, by, bx * lp + layer] = outs[
                n, bx, layer, pl.ds(pl.multiple_of(by * thin, thin), thin)]
        for copy in copies:
            copy.wait_recv()

    def collect(n, step):
        at = pl.ds(pl.multiple_of(bx * R + by * thin, thin), thin)
        copies = []
        for a, b in others:
            to_x, to_y = (bx + a) % nbx, (by + b) % nby
            copies.append(push(
                w_out.at[step, to_y, pl.ds(to_x * lp, lp)], inb.at[n, :, at],
                {"bx": to_x, "by": to_y}))
        for layer in range(lp):
            inb[n, layer, at] = w_out[step, by, bx * lp + layer]
        return copies

    def solve(spectrum, height):
        primes = []
        for l in range(L):
            source = spectrum[l * height:(l + 1) * height] * scale
            if l:
                source = source + inter[l] * primes[-1]
            primes.append(source * coef[l])
        values = [primes[-1]]
        for l in range(L - 2, -1, -1):
            values.insert(0, primes[l] + ratio[l] * values[0])
        return values

    def x_finish(n, dst, height):
        waits = []
        landing = dst.at[pl.ds(group * lp, lp)]
        for t in range(own):
            local = (group + t) % own
            to = part * own + local
            src = outs.at[n, local, :, pl.ds(0, height)]
            if rep == 1:
                if t == 0:
                    continue
                waits.append(push(src, landing, {"bx": to}).wait_recv)
                continue
            slot = fresh()

            def go(src=src, to=to, slot=slot):
                remote(src, landing, {"bx": to}, slot).start()

            def gone(src=src, to=to, slot=slot):
                @pl.when(to != bx)
                def _():
                    remote(src, landing, {"bx": to}, slot).wait_send()

            def came(src=src, to=to, slot=slot, t=t):
                origin = (bx % own + own - t) % own * rep + bx // own

                @pl.when(origin != bx)
                def _():
                    remote(src, landing, {"bx": to}, slot).wait_recv()

            pl.when(to != bx)(go)
            sends.append(gone)
            waits.append(came)

        def keep():
            for layer in range(lp):
                dst[group * lp + layer] = outs[n, bx % own, layer, 0:height]

        if rep == 1:
            keep()
        else:
            pl.when(bx // own == part)(keep)
        for wait in waits:
            wait()

    def y_pass(src, n):
        copies = [push(src, ybuf.at[n, k - 1], {"by": (by + k) % nby}) for k in range(1, nby)]
        total = product(halves(src[...].reshape(L * R, C)), (hy[0, by], hy[1, by]))
        for k in range(1, nby):
            copies[k - 1].wait_recv()
            origin = (by + nby - k) % nby
            total += product(halves(ybuf[n, k - 1].reshape(L * R, C)), (hy[0, origin], hy[1, origin]))
        return total

    def flank_start(rows_too, step, src):
        copies = []
        if rows_too:
            for c in range(3):
                for l in range(L):
                    at = c * L + l
                    row_s[step, 0, at:at + 1] = src[c, l, 0:1]
                    row_s[step, 1, at:at + 1] = src[c, l, R - 1:R]
            col_s[step] = column_tile([src[c, l] for c in range(3) for l in range(L)])
            if step == 0:
                pl.semaphore_wait(barrier, len(greeted))
            copies.append(push(row_s.at[step, 1], row_r.at[step, 0], {"bx": (bx + 1) % nbx}))
            copies.append(push(row_s.at[step, 0], row_r.at[step, 1], {"bx": (bx + nbx - 1) % nbx}))
            tile, land = col_s.at[step], col_r
        else:
            pc_s[step] = column_tile([src[l, 0:R] for l in range(L)])
            tile, land = pc_s.at[step], pc_r
        copies.append(push(tile, land.at[step, 0], {"by": (by + 1) % nby}))
        copies.append(push(tile, land.at[step, 1], {"by": (by + nby - 1) % nby}))
        return copies

    for step in range(STEPS):
        src = p_in if step == 0 else p_mid
        flanks = flank_start(True, step, src)
        if step == 0:
            lateral = lam[...]
            previous = None
            for l in range(L):
                pivot = perm[l] * lateral + inter[l] + inter[l + 1]
                if l:
                    pivot = pivot - inter[l] * previous
                inverse = 1.0 / pivot
                coef[l] = inverse
                previous = inter[l + 1] * inverse
                ratio[l] = previous
        for copy in flanks:
            copy.wait_recv()
        low_col = col_r[step, 0]
        high_col = col_r[step, 1]

        def edges(c, l):
            at = c * L + l
            return (row_r[step, 0, at:at + 1], row_r[step, 1, at:at + 1],
                    low_col[:, C // 2 + at:C // 2 + at + 1], high_col[:, at:at + 1])

        zero = jnp.zeros((R, C), jnp.float32)
        for l in range(L):
            low, high, _, _ = edges(0, l)
            _, _, left, right = edges(1, l)
            along_x, along_y = src[0, l], src[1, l]
            above = src[2, l + 1] if l + 1 < L else zero
            below = src[2, l - 1] if l else zero
            q[step, l] = -0.5 * (
                (x_next(along_x, high) - x_prev(along_x, low))
                + (y_next(along_y, right) - y_prev(along_y, left)) + (above - below))
        copies = x_start(q.at[step], 2 * step)
        if step == 0:
            for load in loads:
                load.wait()
        for l in range(L):
            cells = [src[c, l] for c in range(3)]
            squares = [cell * cell for cell in cells]
            whole = squares[0] + squares[1] + squares[2]
            for c in range(3):
                cell, square = cells[c], squares[c]
                low, high, left, right = edges(c, l)
                above = src[c, l + 1] if l + 1 < L else zero
                below = src[c, l - 1] if l else zero
                smooth = stiff[l] * (
                    (x_next(cell, high) + x_prev(cell, low) + y_next(cell, right)
                     + y_prev(cell, left) - 4.0 * cell) + (above + below - 2.0 * cell))
                drive = cell * (
                    2.0 * alpha[l] + 4.0 * landau[0, l] * square
                    + 2.0 * landau[1, l] * (whole - square)
                    + 6.0 * landau[2, l] * (square * square))
                base[c, l] = cell - step_size * (drive - smooth)
        n = 2 * step
        x_mix(copies, n)
        if wide:
            spread(n, step)
            table = (hy[0], hy[1])
            full = jnp.concatenate(
                [z_in[step, j].reshape(L * thin, C) for j in range(nby)], axis=1)
            values = solve(product(halves(full), table), thin)
            full = product(halves(jnp.concatenate(values, axis=0)), table)
            for j in range(nby):
                w_out[step, j] = full[:, j * C:(j + 1) * C].reshape(L, thin, C)
            copies = collect(n + 1, step)
        else:
            x_finish(n, rec_f.at[step], R)
            for l, value in enumerate(solve(y_pass(rec_f.at[step], n), R)):
                phat[step, l] = value
            u[step] = y_pass(phat.at[step], n + 1).reshape(L, R, C)
            copies = x_start(u.at[step], n + 1)
        x_mix(copies, n + 1)
        x_finish(n + 1, rec_i.at[step], R2)
        flanks = flank_start(False, step, rec_i.at[step])
        last = step == STEPS - 1
        target = p_out if last else p_mid
        for l in range(L):
            phi = rec_i[step, l, 0:R]
            low = rec_i[step, l, R:R + 1]
            high = rec_i[step, l, R + 1:R + 2]
            along_x = -0.5 * (x_next(phi, high) - x_prev(phi, low))
            above = rec_i[step, l + 1, 0:R] if l + 1 < L else zero
            below = rec_i[step, l - 1, 0:R] if l else zero
            along_z = -0.5 * (above - below)
            target[0, l] = base[0, l] + step_size * along_x
            target[2, l] = base[2, l] + step_size * along_z
            if last:
                f_out[0, l] = along_x
                f_out[2, l] = along_z
        for copy in flanks:
            copy.wait_recv()
        low_phi = pc_r[step, 0]
        high_phi = pc_r[step, 1]
        for l in range(L):
            phi = rec_i[step, l, 0:R]
            along_y = -0.5 * (y_next(phi, high_phi[:, l:l + 1])
                              - y_prev(phi, low_phi[:, C // 2 + l:C // 2 + l + 1]))
            target[1, l] = base[1, l] + step_size * along_y
            if last:
                f_out[1, l] = along_y
    for wait in sends:
        wait()


def shards(polarization, alpha_field, landau, stiffness, permittivity, interfaces):
    _, L, R, C = polarization.shape
    nbx = lax.axis_size("bx")
    nby = lax.axis_size("by")
    bx = lax.axis_index("bx")
    by = lax.axis_index("by")
    rep = max(1, nbx // L)
    lp = max(1, L // nbx)
    own = nbx // rep
    grid_x, grid_y = nbx * R, nby * C
    R2 = R + PAD
    wide = is_wide(R, nbx, nby, L)
    pool = np if wide else jnp
    make = fixed_table if wide else cas_table
    line = pool.arange(R2, dtype=jnp.int32)
    line = pool.where(line < R, line, pool.where(line == R, -1, R))
    owners = pool.arange(own, dtype=jnp.int32)
    if not wide:
        owners = owners + bx % rep * own
    wanted = ((owners[:, None] * R + line[None, :] + grid_x) % grid_x).reshape(own * R2, 1)
    hx = make(wanted, pool.arange(grid_x, dtype=jnp.int32)[None, :], grid_x)
    every_col = pool.arange(grid_y, dtype=jnp.int32)
    my_rows = bx * R + jnp.arange(R, dtype=jnp.int32)
    my_cols = by * C + jnp.arange(C, dtype=jnp.int32)
    if wide:
        hy = make(every_col[:, None], every_col[None, :], grid_y)
        my_rows = bx * R + by * (R // nby) + jnp.arange(R // nby, dtype=jnp.int32)
        my_cols = jnp.arange(grid_y, dtype=jnp.int32)
    else:
        hy = make(every_col[:, None], my_cols[None, :], grid_y).reshape(2, nby, C, C)
    wave_x = jnp.sin(jnp.pi * my_rows.astype(jnp.float32) / grid_x)
    wave_y = jnp.sin(jnp.pi * my_cols.astype(jnp.float32) / grid_y)
    lam = 4.0 * wave_x[:, None] ** 2 + 4.0 * wave_y[None, :] ** 2
    sizes = (L, R, C, nbx, nby, rep, lp, own)
    n_copies = STEPS * (6 + 2 * (nbx * nby + own if wide else nbx + own + nby))
    f32 = jnp.float32
    vmem = pl.BlockSpec(memory_space=pltpu.VMEM)
    hbm = pl.BlockSpec(memory_space=pltpu.HBM)
    smem = pl.BlockSpec(memory_space=pltpu.SMEM)
    S = STEPS
    scratch = [
        pltpu.VMEM((3, L, R, C), f32), pltpu.VMEM((3, L, R, C), f32),
        pltpu.VMEM((L,) + lam.shape, f32), pltpu.VMEM((L,) + lam.shape, f32),
        pltpu.VMEM((S, L, R, C), f32), pltpu.VMEM((2 * S, lp, grid_x, C), f32),
        pltpu.VMEM((2 * S, own, lp, R2, C), f32), pltpu.VMEM((S, L, R2, C), f32),
        pltpu.VMEM((S, 2, 3 * L, C), f32), pltpu.VMEM((S, 2, 3 * L, C), f32),
        pltpu.VMEM((S, R, C), f32), pltpu.VMEM((S, 2, R, C), f32),
        pltpu.VMEM((S, R, C), f32), pltpu.VMEM((S, 2, R, C), f32),
        pltpu.SemaphoreType.DMA((n_copies,)), pltpu.SemaphoreType.DMA((n_copies,)),
        pltpu.VMEM((L, R, C), f32), pltpu.VMEM(hx.shape, hx.dtype),
        pltpu.VMEM(hy.shape, hy.dtype), pltpu.SemaphoreType.DMA((3,)),
    ]
    if wide:
        thin = (S, nby, L, R // nby, C)
        scratch += [pltpu.VMEM(thin, f32), pltpu.VMEM(thin, f32)]
    else:
        scratch += [
            pltpu.VMEM((S, L, R, C), f32), pltpu.VMEM((2 * S, nby - 1, L, R, C), f32),
            pltpu.VMEM((S, L, R, C), f32), pltpu.VMEM((S, L, R, C), f32),
        ]
    out = jax.ShapeDtypeStruct(polarization.shape, f32)
    return pl.pallas_call(
        functools.partial(kernel, sizes),
        out_shape=(out, out),
        in_specs=[vmem, hbm, smem, smem, smem, smem, vmem, hbm, hbm],
        out_specs=(vmem, vmem),
        scratch_shapes=scratch,
        compiler_params=pltpu.CompilerParams(
            collective_id=0, has_side_effects=True, vmem_limit_bytes=65 * 1000 * 1000),
    )(polarization, alpha_field, landau, stiffness, permittivity, interfaces, lam, hx, hy)


def solution(mesh):
    return jax.shard_map(
        shards,
        mesh=mesh,
        in_specs=(P(None, None, "bx", "by"), P(None, "bx", "by"), P(), P(), P(), P()),
        out_specs=(P(None, None, "bx", "by"), P(None, None, "bx", "by")),
        check_vma=False,
    )
```

profile of v0, /device:TPU:0, one launch (start us, length us, event | category | flops | bytes accessed | tf_op | source)
XLA Modules:
  0.0 74.0 jit_solution(17915008343972579319)
XLA Ops:
  0.7 0.7 broadcast_add_fusion.lam
  1.4 70.0 %shard_map.95 = (f32[3,8,32,128]{3,2,1,0:T(8,128)}, f32[3,8,32,128]{3,2,1,0:T(8,128)}) custom-call(f32[3,8,32,128]{3,2,1,0:T(8,128)} %p_in.1, f32[8,32,128]{2,1,0:T(8,128)} %alpha_h.1, f32[3,8]{1,0:T(4,128)} %landau.1, f32[8]{0:T(128)} %stiff.1, f32[8]{0:T(128)} %perm.1, f32[9]{0:T(128)} %inter.1, f32[8,512]{1,0:T(8,128)} %broadcast_add_fusion.lam, ...), custom_call_target="tpu_custom_call" | custom-call | tf_op jit(solution)/shard_map/pallas_call | solution.py:412
  71.5 0.0 copy-start
  71.5 1.8 %copy.12 = f32[3,8,32,128]{3,2,1,0:T(8,128)} copy(f32[3,8,32,128]{3,2,1,0:T(8,128)} %get-tuple-element.4) | data formatting | bytes 786432
  73.3 0.0 copy-done
  73.3 0.7 %copy.13 = f32[3,8,32,128]{3,2,1,0:T(8,128)} copy(f32[3,8,32,128]{3,2,1,0:T(8,128)S(1)} %copy-done) | data formatting | bytes 786432
  (2 shorter events, 0.1 us)
Async XLA Ops:
  71.5 1.8 %copy-start = (f32[3,8,32,128]{3,2,1,0:T(8,128)S(1)}, f32[3,8,32,128]{3,2,1,0:T(8,128)}, u32[]{:S(2)}) copy-start(f32[3,8,32,128]{3,2,1,0:T(8,128)} %get-tuple-element.5) | copy-start | bytes 1179652
where the time goes:
time: 75.2 us; the launch traced here: 74 us
  Pallas kernels  70 us (93%)
  local copies, waits for them, and re-layouts  2.57 us (3%)
  other arithmetic  0.77 us (1%)
    pallas_call x1, Pallas kernels, shards(): pl.pallas_call(functools.partial(kernel, sizes), out_shape=(out, out), in...  70 us
    unnamed x4, local copies, waits for them, and re-layouts  2.57 us

commit v1 on v0

--- a/solution.py
+++ b/solution.py
@@ -420,9 +420,445 @@
     )(polarization, alpha_field, landau, stiffness, permittivity, interfaces, lam, hx, hy)
 
 
+def fits(L, R, C, nbx, nby):
+    slab = R // nby
+    return (L == nbx and slab == 8 and slab * nby == R and nby > 1 and C % L == 0
+            and L & (L - 1) == 0)
+
+
+def join(parts, axis):
+    return jnp.concatenate(parts, axis=axis)
+
+
+def fused(sizes, p_in, alpha_h, landau, stiff, perm, inter, wx_h, wy_h, hx_h, hy_h,
+          p_out, f_out, *scratch):
+    L, R, C, nbx, nby = sizes
+    (p_mid, base, coef, ratio, a_s, a_r, b_s, b_r, c_s, c_r, d_s, d_r,
+     row_s, row_r, col_s, col_r, ssem, rsem, alpha, wx, wy, hx, hy, local_sem) = scratch
+    slab = R // nby
+    per = C // L
+    NX, NY = nbx * R, nby * C
+    thick = slab + 1
+    bx = lax.axis_index("bx")
+    by = lax.axis_index("by")
+    scale = 1.0 / (NX * NY)
+    f32 = jnp.float32
+    dot = functools.partial(jnp.dot, preferred_element_type=f32)
+    mine = pl.multiple_of((bx * nby + by) * per, per)
+    loads = [pltpu.make_async_copy(src, dst, local_sem.at[at]) for at, (src, dst) in enumerate((
+        (alpha_h, alpha), (wx_h, wx), (wy_h.at[pl.ds(mine, per)], wy), (hx_h, hx), (hy_h, hy)))]
+    for load in loads:
+        load.start()
+    slots = [0]
+    sends = []
+
+    barrier = pltpu.get_barrier_semaphore()
+    others = [(a, b) for b in range(nby) for a in range(nbx) if a or b]
+    for a, b in others:
+        pl.semaphore_signal(
+            barrier, inc=1, device_id={"bx": (bx + a) % nbx, "by": (by + b) % nby},
+            device_id_type=MESH)
+
+    def push(src, dst, device):
+        slot = slots[0]
+        slots[0] += 1
+        copy = pltpu.make_async_remote_copy(
+            src_ref=src, dst_ref=dst, send_sem=ssem.at[slot], recv_sem=rsem.at[slot],
+            device_id=device, device_id_type=MESH)
+        copy.start()
+        sends.append(copy.wait_send)
+        return copy
+
+    rows = lax.broadcasted_iota(jnp.int32, (R, C), 0)
+    lanes = lax.broadcasted_iota(jnp.int32, (R, C), 1)
+    rows8 = lax.broadcasted_iota(jnp.int32, (slab, C), 0)
+    lanes8 = lax.broadcasted_iota(jnp.int32, (slab, C), 1)
+    zero = jnp.zeros((R, C), f32)
+    zero8 = jnp.zeros((slab, C), f32)
+
+    def x_next(f, high):
+        return jnp.where(rows == R - 1, high, pltpu.roll(f, R - 1, 0))
+
+    def x_prev(f, low):
+        return jnp.where(rows == 0, low, pltpu.roll(f, 1, 0))
+
+    def y_next(f, high):
+        return jnp.where(lanes == C - 1, high, pltpu.roll(f, C - 1, 1))
+
+    def y_prev(f, low):
+        return jnp.where(lanes == 0, low, pltpu.roll(f, 1, 1))
+
+    def charge(n, src):
+        edge = zero
+        for l in range(L):
+            along_x, along_y = src[0, l], src[1, l]
+            above = src[2, l + 1] if l + 1 < L else zero
+            below = src[2, l - 1] if l else zero
+            value = -0.5 * ((x_next(along_x, 0.0) - x_prev(along_x, 0.0))
+                            + (y_next(along_y, 0.0) - y_prev(along_y, 0.0)) + (above - below))
+            for j in range(nby):
+                a_s[n, j, l] = value[j * slab:(j + 1) * slab]
+            a_s[n, 0, L + 1, l:l + 1] = -0.5 * along_x[0:1]
+            a_s[n, nby - 1, L + 1, l:l + 1] = 0.5 * along_x[R - 1:R]
+            edge = jnp.where(lanes == l, -0.5 * along_y[:, 0:1], edge)
+            edge = jnp.where(lanes == L + l, 0.5 * along_y[:, C - 1:C], edge)
+        for j in range(nby):
+            a_s[n, j, L] = edge[j * slab:(j + 1) * slab]
+            if 0 < j < nby - 1:
+                a_s[n, j, L + 1] = jnp.zeros((L, C), f32)
+
+    def among_y(source, landing, n):
+        copies = []
+        for b in range(1, nby):
+            to = (by + b) % nby
+            copies.append(push(source.at[n, to], landing.at[n, by], {"by": to}))
+        landing[n, by] = source[n, by]
+        return copies
+
+    def wait(copies):
+        for copy in copies:
+            copy.wait_recv()
+
+    def spread(source, landing, n, flip):
+        part = pl.ds(0, thick)
+        copies = []
+        for a, b in others:
+            to_x, to_y = (bx + a) % nbx, (by + b) % nby
+            if flip:
+                src, dst = source.at[n, to_x, to_y, part], landing.at[n, by, bx, part]
+            else:
+                src, dst = source.at[n, to_y, to_x, part], landing.at[n, bx, by, part]
+            copies.append(push(src, dst, {"bx": to_x, "by": to_y}))
+        if flip:
+            landing[n, by, bx, 0:thick] = source[n, bx, by, 0:thick]
+        else:
+            landing[n, bx, by, 0:thick] = source[n, by, bx, 0:thick]
+        return copies
+
+    def swap_groups(tiles):
+        height = tiles[0].shape[0]
+        group = lax.broadcasted_iota(jnp.int32, (height, C), 1) // per
+        tiles = list(tiles)
+        s = 1
+        while s < L:
+            upper = group % (2 * s) >= s
+            for at in range(L):
+                if at % (2 * s) < s:
+                    low, high = tiles[at], tiles[at + s]
+                    tiles[at] = jnp.where(upper, pltpu.roll(high, s * per, 1), low)
+                    tiles[at + s] = jnp.where(upper, high, pltpu.roll(low, C - s * per, 1))
+            s *= 2
+        return tiles
+
+    def swap_rows(tile):
+        group = lanes8 // per
+        s = 1
+        while s < L:
+            upper = group % (2 * s) >= s
+            later = rows8 % (2 * s) >= s
+            ahead = pltpu.roll(pltpu.roll(tile, L - s, 0), s * per, 1)
+            behind = pltpu.roll(pltpu.roll(tile, s, 0), C - s * per, 1)
+            tile = jnp.where(later, jnp.where(upper, tile, behind), jnp.where(upper, ahead, tile))
+            s *= 2
+        return tile
+
+    def y_table(full):
+        height = full.shape[0]
+        high = full.astype(jnp.bfloat16)
+        wide = high.astype(f32)
+        both = join([wide, full - wide], 0).astype(jnp.bfloat16)
+        first = dot(both, hy[0])
+        return first[:height] + first[height:] + dot(high, hy[1])
+
+    def y_forward(n):
+        columns = []
+        for j in range(nby):
+            from_left = a_r[n, (j + nby - 1) % nby, L]
+            from_right = a_r[n, (j + 1) % nby, L]
+            tiles = []
+            for l in range(L):
+                extra = jnp.where(
+                    lanes8 == 0, from_left[:, L + l:L + l + 1],
+                    jnp.where(lanes8 == C - 1, from_right[:, l:l + 1], 0.0))
+                tiles.append(a_r[n, j, l] + extra)
+            columns.append(join(tiles + [a_r[n, j, L + 1], zero8], 0))
+        out = y_table(join(columns, 1))
+        tiles = [join([out[l * slab:(l + 1) * slab, t * C:(t + 1) * C] for t in range(nby)], 0)
+                 for l in range(L)]
+        tiles = swap_groups(tiles)
+        for t in range(nby):
+            halo = swap_rows(out[L * slab:L * slab + L, t * C:(t + 1) * C])
+            for e in range(L):
+                b_s[n, t, e, 0:slab] = tiles[e][t * slab:(t + 1) * slab]
+                b_s[n, t, e, slab:thick] = halo[e:e + 1]
+
+    def y_backward(n):
+        tiles = swap_groups([join([c_r[n, t, e, 0:slab] for t in range(nby)], 0)
+                             for e in range(L)])
+        halos = [swap_rows(join([c_r[n, t, e, slab:thick] for e in range(L)], 0))
+                 for t in range(nby)]
+        lines = [join([tiles[l][t * slab:(t + 1) * slab] for t in range(nby)], 1)
+                 for l in range(L)]
+        lines += [join(halos, 1), jnp.zeros((slab, NY), f32)]
+        out = y_table(join(lines, 0))
+        for j in range(nby):
+            edge = zero8
+            left, right = (j + nby - 1) % nby, (j + 1) % nby
+            for l in range(L):
+                line = out[l * slab:(l + 1) * slab]
+                d_s[n, j, l] = line[:, j * C:(j + 1) * C]
+                edge = jnp.where(lanes8 == l, line[:, left * C + C - 1:left * C + C], edge)
+                edge = jnp.where(lanes8 == L + l, line[:, right * C:right * C + 1], edge)
+            d_s[n, j, L] = edge
+            d_s[n, j, L + 1] = out[L * slab:L * slab + L, j * C:(j + 1) * C]
+
+    def spectrum(n):
+        tiles = []
+        for i in range(nbx):
+            for j in range(nby):
+                tile = b_r[n, i, j, 0:slab]
+                if j == 0:
+                    tile = tile + jnp.where(
+                        rows8 == 0, b_r[n, (i + nbx - 1) % nbx, nby - 1, slab:thick], 0.0)
+                if j == nby - 1:
+                    tile = tile + jnp.where(
+                        rows8 == slab - 1, b_r[n, (i + 1) % nbx, 0, slab:thick], 0.0)
+                tiles.append(tile)
+        full = join(tiles, 0).T
+        high = full.astype(jnp.bfloat16)
+        wide = high.astype(f32)
+        both = join([wide, full - wide], 0).astype(jnp.bfloat16)
+        first = dot(both, hx[0])
+        out = (first[:C] + first[C:] + dot(high, hx[1])) * scale
+        return [out[l * per:(l + 1) * per] for l in range(L)]
+
+    def solve(sources):
+        primes = []
+        for l in range(L):
+            source = sources[l]
+            if l:
+                source = source + inter[l] * primes[-1]
+            primes.append(source * coef[l])
+        values = [primes[-1]]
+        for l in range(L - 2, -1, -1):
+            values.insert(0, primes[l] + ratio[l] * values[0])
+        return values
+
+    def x_backward(n, values):
+        high, low = halves(join(values, 0))
+        turn = functools.partial(
+            lax.dot_general, dimension_numbers=(((1,), (1,)), ((), ())),
+            preferred_element_type=f32)
+        first = turn(hx[...].reshape(2 * NX, NX), high)
+        out = first[:NX] + first[NX:] + turn(hx[0], low)
+        for i in range(nbx):
+            for j in range(nby):
+                at = i * R + j * slab
+                c_s[n, i, j, 0:slab] = out[at:at + slab]
+                if j == 0:
+                    line = (at + NX - 1) % NX
+                else:
+                    line = (at + slab) % NX
+                c_s[n, i, j, slab:thick] = out[line:line + 1]
+
+    def flank_start(n, src):
+        tile = zero
+        for c in range(3):
+            for l in range(L):
+                at = c * L + l
+                cell = src[c, l]
+                row_s[n, 0, at:at + 1] = cell[0:1]
+                row_s[n, 1, at:at + 1] = cell[R - 1:R]
+                tile = jnp.where(lanes == at, cell[:, 0:1], tile)
+                tile = jnp.where(lanes == C // 2 + at, cell[:, C - 1:C], tile)
+        col_s[n] = tile
+
+    def flank_send(n):
+        return [
+            push(row_s.at[n, 1], row_r.at[n, 0], {"bx": (bx + 1) % nbx}),
+            push(row_s.at[n, 0], row_r.at[n, 1], {"bx": (bx + nbx - 1) % nbx}),
+            push(col_s.at[n], col_r.at[n, 0], {"by": (by + 1) % nby}),
+            push(col_s.at[n], col_r.at[n, 1], {"by": (by + nby - 1) % nby})]
+
+    def relax_inside(src):
+        for l in range(L):
+            cells = [src[c, l] for c in range(3)]
+            squares = [cell * cell for cell in cells]
+            whole = squares[0] + squares[1] + squares[2]
+            for c in range(3):
+                cell, square = cells[c], squares[c]
+                above = src[c, l + 1] if l + 1 < L else zero
+                below = src[c, l - 1] if l else zero
+                smooth = stiff[l] * (
+                    (x_next(cell, 0.0) + x_prev(cell, 0.0) + y_next(cell, 0.0)
+                     + y_prev(cell, 0.0) - 4.0 * cell) + (above + below - 2.0 * cell))
+                drive = cell * (
+                    2.0 * alpha[l] + 4.0 * landau[0, l] * square
+                    + 2.0 * landau[1, l] * (whole - square)
+                    + 6.0 * landau[2, l] * (square * square))
+                base[c, l] = cell - step_size * (drive - smooth)
+
+    def relax_edges(n):
+        low_col = col_r[n, 0]
+        high_col = col_r[n, 1]
+        for l in range(L):
+            weight = step_size * stiff[l]
+            for c in range(3):
+                at = c * L + l
+                add = jnp.where(lanes == 0, low_col[:, C // 2 + at:C // 2 + at + 1], 0.0)
+                add = add + jnp.where(lanes == C - 1, high_col[:, at:at + 1], 0.0)
+                add = add + jnp.where(rows == 0, row_r[n, 0, at:at + 1], 0.0)
+                add = add + jnp.where(rows == R - 1, row_r[n, 1, at:at + 1], 0.0)
+                base[c, l] += weight * add
+
+    def field(n):
+        edge = join([d_r[n, j, L] for j in range(nby)], 0)
+        phis = [join([d_r[n, j, l] for j in range(nby)], 0) for l in range(L)]
+        for l in range(L):
+            phi = phis[l]
+            low = d_r[n, 0, L + 1, l:l + 1]
+            high = d_r[n, nby - 1, L + 1, l:l + 1]
+            along_x = -0.5 * (x_next(phi, high) - x_prev(phi, low))
+            along_y = -0.5 * (y_next(phi, edge[:, L + l:L + l + 1])
+                              - y_prev(phi, edge[:, l:l + 1]))
+            above = phis[l + 1] if l + 1 < L else zero
+            below = phis[l - 1] if l else zero
+            yield l, (along_x, along_y, -0.5 * (above - below))
+
+    charge(0, p_in)
+    flank_start(0, p_in)
+    pl.semaphore_wait(barrier, len(others))
+    first_a = among_y(a_s, a_r, 0)
+    flanks = flank_send(0)
+    loads[0].wait()
+    relax_inside(p_in)
+    loads[1].wait()
+    loads[2].wait()
+    wave_x = wx[0:1]
+    wave_y = join([wy[...]] * (NX // C), 1)
+    lateral = wave_x + wave_y
+    previous = None
+    for l in range(L):
+        pivot = perm[l] * lateral + inter[l] + inter[l + 1]
+        if l:
+            pivot = pivot - inter[l] * previous
+        inverse = 1.0 / pivot
+        coef[l] = inverse
+        previous = inter[l + 1] * inverse
+        ratio[l] = previous
+    loads[3].wait()
+    loads[4].wait()
+    wait(first_a)
+    y_forward(0)
+    first_b = spread(b_s, b_r, 0, False)
+    wait(flanks)
+    relax_edges(0)
+    charge(1, base)
+    second_a = among_y(a_s, a_r, 1)
+    wait(second_a)
+    y_forward(1)
+    second_b = spread(b_s, b_r, 1, False)
+    wait(first_b)
+    values = solve(spectrum(0))
+    x_backward(0, values)
+    first_c = spread(c_s, c_r, 0, True)
+    bend = -(wave_x * (1.0 - 0.25 * wave_x) + wave_y * (1.0 - 0.25 * wave_y))
+    slopes = []
+    none = jnp.zeros_like(values[0])
+    for l in range(L):
+        above = values[l + 1] if l + 1 < L else none
+        below = values[l - 1] if l else none
+        slopes.append(0.5 * (above - below))
+    moved = []
+    for l in range(L):
+        above = slopes[l + 1] if l + 1 < L else none
+        below = slopes[l - 1] if l else none
+        moved.append(step_size * (bend * values[l] + 0.5 * (above - below)))
+    wait(second_b)
+    x_backward(1, solve([here + more for here, more in zip(spectrum(1), moved)]))
+    second_c = spread(c_s, c_r, 1, True)
+    wait(first_c)
+    y_backward(0)
+    first_d = among_y(d_s, d_r, 0)
+    wait(first_d)
+    for l, parts in field(0):
+        for c in range(3):
+            p_mid[c, l] = base[c, l] + step_size * parts[c]
+    flank_start(1, p_mid)
+    flanks = flank_send(1)
+    wait(second_c)
+    y_backward(1)
+    second_d = among_y(d_s, d_r, 1)
+    relax_inside(p_mid)
+    wait(flanks)
+    relax_edges(1)
+    wait(second_d)
+    for l, parts in field(1):
+        for c in range(3):
+            f_out[c, l] = parts[c]
+            p_out[c, l] = base[c, l] + step_size * parts[c]
+    for send in sends:
+        send()
+
+
+def fused_shards(polarization, alpha_field, landau, stiffness, permittivity, interfaces):
+    _, L, R, C = polarization.shape
+    nbx = lax.axis_size("bx")
+    nby = lax.axis_size("by")
+    grid_x, grid_y = nbx * R, nby * C
+    per = C // L
+    line = np.arange(grid_x)
+    hx = fixed_table(line[:, None], line[None, :], grid_x)
+    line = np.arange(grid_y)
+    hy = fixed_table(line[:, None], line[None, :], grid_y)
+    wave_x = 4.0 * np.sin(np.pi * np.arange(grid_x) / grid_x) ** 2
+    wave_x = jnp.asarray(np.tile(wave_x[None, :], (8, 1)).astype(np.float32))
+    at = np.arange(nbx * nby)
+    first = (at % nby) * C + (at // nby) * per
+    mode = (first[:, None] + np.arange(per)[None, :]).reshape(-1)
+    wave_y = 4.0 * np.sin(np.pi * mode / grid_y) ** 2
+    wave_y = jnp.asarray(np.tile(wave_y[:, None], (1, C)).astype(np.float32))
+    f32 = jnp.float32
+    vmem = pl.BlockSpec(memory_space=pltpu.VMEM)
+    hbm = pl.BlockSpec(memory_space=pltpu.HBM)
+    smem = pl.BlockSpec(memory_space=pltpu.SMEM)
+    S = 2
+    n_copies = S * (4 + 2 * (nby - 1) + 2 * (nbx * nby - 1))
+    by_y = pltpu.VMEM((S, nby, L + 2, 8, C), f32)
+    by_mode = pltpu.VMEM((S, nby, nbx, 16, C), f32)
+    by_place = pltpu.VMEM((S, nbx, nby, 16, C), f32)
+    scratch = [
+        pltpu.VMEM((3, L, R, C), f32), pltpu.VMEM((3, L, R, C), f32),
+        pltpu.VMEM((L, per, grid_x), f32), pltpu.VMEM((L, per, grid_x), f32),
+        by_y, by_y, by_mode, by_place, by_place, by_mode, by_y, by_y,
+        pltpu.VMEM((S, 2, 3 * L, C), f32), pltpu.VMEM((S, 2, 3 * L, C), f32),
+        pltpu.VMEM((S, R, C), f32), pltpu.VMEM((S, 2, R, C), f32),
+        pltpu.SemaphoreType.DMA((n_copies,)), pltpu.SemaphoreType.DMA((n_copies,)),
+        pltpu.VMEM((L, R, C), f32), pltpu.VMEM(wave_x.shape, f32), pltpu.VMEM((per, C), f32),
+        pltpu.VMEM(hx.shape, hx.dtype), pltpu.VMEM(hy.shape, hy.dtype),
+        pltpu.SemaphoreType.DMA((5,)),
+    ]
+    out = jax.ShapeDtypeStruct(polarization.shape, f32)
+    return pl.pallas_call(
+        functools.partial(fused, (L, R, C, nbx, nby)),
+        out_shape=(out, out),
+        in_specs=[vmem, hbm, smem, smem, smem, smem, hbm, hbm, hbm, hbm],
+        out_specs=(vmem, vmem),
+        scratch_shapes=scratch,
+        compiler_params=pltpu.CompilerParams(
+            collective_id=0, has_side_effects=True, vmem_limit_bytes=60 * 1000 * 1000),
+    )(polarization, alpha_field, landau, stiffness, permittivity, interfaces,
+      wave_x, wave_y, hx, hy)
+
+
 def solution(mesh):
+    def run(polarization, *rest):
+        _, L, R, C = polarization.shape
+        body = fused_shards if fits(L, R, C, lax.axis_size("bx"), lax.axis_size("by")) else shards
+        return body(polarization, *rest)
+
     return jax.shard_map(
-        shards,
+        run,
         mesh=mesh,
         in_specs=(P(None, None, "bx", "by"), P(None, "bx", "by"), P(), P(), P(), P()),
         out_specs=(P(None, None, "bx", "by"), P(None, None, "bx", "by")),

time: 75.2 us -> 43.6 us (0.58); the launches traced: 74 us -> 43.4 us
  Pallas kernels: 70 us -> 40.2 us
  other arithmetic: 0.77 us -> 0 us
    pallas_call x1, Pallas kernels: 70 us -> 40.2 us  [fused_shards(): pl.pallas_call(functools.partial(fused, (L, R, C, nbx, nby)), out_shape=(...]
where the time goes in v1:
time: 43.6 us; the launch traced here: 43.4 us
  Pallas kernels  40.2 us (92%)
  local copies, waits for them, and re-layouts  2.57 us (6%)
  between operations  0.65 us (1%)
    pallas_call x1, Pallas kernels, fused_shards(): pl.pallas_call(functools.partial(fused, (L, R, C, nbx, nby)), out_shape=(...  40.2 us
    unnamed x4, local copies, waits for them, and re-layouts  2.57 us

profile of v1, /device:TPU:0, one launch (start us, length us, event | category | flops | bytes accessed | tf_op | source)
XLA Modules:
  0.0 43.4 jit_solution(9314084277369508687)
XLA Ops:
  0.6 40.2 %shard_map.113 = (f32[3,8,32,128]{3,2,1,0:T(8,128)}, f32[3,8,32,128]{3,2,1,0:T(8,128)}) custom-call(f32[3,8,32,128]{3,2,1,0:T(8,128)} %p_in.1, f32[8,32,128]{2,1,0:T(8,128)} %alpha_h.1, f32[3,8]{1,0:T(4,128)} %landau.1, f32[8]{0:T(128)} %stiff.1, f32[8]{0:T(128)} %perm.1, f32[9]{0:T(128)} %inter.1, f32[8,256]{1,0:T(8,128)} %constant.10.clone.wx_h, ...), custom_call_target="tpu_custom_call" | custom-call | tf_op jit(solution)/shard_map/pallas_call | solution.py:842
  40.9 0.0 copy-start
  40.9 1.8 %copy.14 = f32[3,8,32,128]{3,2,1,0:T(8,128)} copy(f32[3,8,32,128]{3,2,1,0:T(8,128)} %get-tuple-element.4) | data formatting | bytes 786432
  42.7 0.0 copy-done
  42.7 0.7 %copy.15 = f32[3,8,32,128]{3,2,1,0:T(8,128)} copy(f32[3,8,32,128]{3,2,1,0:T(8,128)S(1)} %copy-done) | data formatting | bytes 786432
Async XLA Ops:
  40.9 1.8 %copy-start = (f32[3,8,32,128]{3,2,1,0:T(8,128)S(1)}, f32[3,8,32,128]{3,2,1,0:T(8,128)}, u32[]{:S(2)}) copy-start(f32[3,8,32,128]{3,2,1,0:T(8,128)} %get-tuple-element.5) | copy-start | bytes 1179652

commit v2 on v1

--- a/solution.py
+++ b/solution.py
@@ -423,18 +423,28 @@
 def fits(L, R, C, nbx, nby):
     slab = R // nby
     return (L == nbx and slab == 8 and slab * nby == R and nby > 1 and C % L == 0
-            and L & (L - 1) == 0)
+            and nbx & (nbx - 1) == 0 and nby & (nby - 1) == 0)
+
+
+def partner(index, mask, size):
+    other = 0
+    bit = 1
+    while bit < size:
+        here = index // bit % 2
+        other = other + bit * (1 - here if mask // bit % 2 else here)
+        bit *= 2
+    return other
 
 
 def join(parts, axis):
     return jnp.concatenate(parts, axis=axis)
 
 
-def fused(sizes, p_in, alpha_h, landau, stiff, perm, inter, wx_h, wy_h, hx_h, hy_h,
-          p_out, f_out, *scratch):
+def fused(sizes, p_h, alpha_h, landau, stiff, perm, inter, wx_h, wy_h, hx_h, hy_h,
+          base_o, down_o, *scratch):
     L, R, C, nbx, nby = sizes
     (p_mid, base, coef, ratio, a_s, a_r, b_s, b_r, c_s, c_r, d_s, d_r,
-     row_s, row_r, col_s, col_r, ssem, rsem, alpha, wx, wy, hx, hy, local_sem) = scratch
+     row_s, row_r, col_s, col_r, ssem, rsem, p_in, alpha, wx, wy, hx, hy, local_sem) = scratch
     slab = R // nby
     per = C // L
     NX, NY = nbx * R, nby * C
@@ -444,20 +454,23 @@
     scale = 1.0 / (NX * NY)
     f32 = jnp.float32
     dot = functools.partial(jnp.dot, preferred_element_type=f32)
+    slots = [0]
+    sends = []
+
+    barrier = pltpu.get_barrier_semaphore()
+    at_x = [partner(bx, a, nbx) for a in range(nbx)]
+    at_y = [partner(by, b, nby) for b in range(nby)]
+    others = [(a, b) for b in range(nby) for a in range(nbx) if a or b]
+    others.sort(key=lambda ab: -(ab[0] // 2 + ab[0] % 2 + ab[1] // 2))
+    for a, b in others:
+        pl.semaphore_signal(
+            barrier, inc=1, device_id={"bx": at_x[a], "by": at_y[b]}, device_id_type=MESH)
     mine = pl.multiple_of((bx * nby + by) * per, per)
     loads = [pltpu.make_async_copy(src, dst, local_sem.at[at]) for at, (src, dst) in enumerate((
-        (alpha_h, alpha), (wx_h, wx), (wy_h.at[pl.ds(mine, per)], wy), (hx_h, hx), (hy_h, hy)))]
+        (p_h, p_in), (alpha_h, alpha), (wx_h, wx), (wy_h.at[pl.ds(mine, per)], wy), (hx_h, hx),
+        (hy_h, hy)))]
     for load in loads:
         load.start()
-    slots = [0]
-    sends = []
-
-    barrier = pltpu.get_barrier_semaphore()
-    others = [(a, b) for b in range(nby) for a in range(nbx) if a or b]
-    for a, b in others:
-        pl.semaphore_signal(
-            barrier, inc=1, device_id={"bx": (bx + a) % nbx, "by": (by + b) % nby},
-            device_id_type=MESH)
 
     def push(src, dst, device):
         slot = slots[0]
@@ -509,8 +522,8 @@
 
     def among_y(source, landing, n):
         copies = []
-        for b in range(1, nby):
-            to = (by + b) % nby
+        for b in range(nby - 1, 0, -1):
+            to = at_y[b]
             copies.append(push(source.at[n, to], landing.at[n, by], {"by": to}))
         landing[n, by] = source[n, by]
         return copies
@@ -523,7 +536,7 @@
         part = pl.ds(0, thick)
         copies = []
         for a, b in others:
-            to_x, to_y = (bx + a) % nbx, (by + b) % nby
+            to_x, to_y = at_x[a], at_y[b]
             if flip:
                 src, dst = source.at[n, to_x, to_y, part], landing.at[n, by, bx, part]
             else:
@@ -698,7 +711,7 @@
                     + 6.0 * landau[2, l] * (square * square))
                 base[c, l] = cell - step_size * (drive - smooth)
 
-    def relax_edges(n):
+    def relax_edges(n, target):
         low_col = col_r[n, 0]
         high_col = col_r[n, 1]
         for l in range(L):
@@ -709,7 +722,7 @@
                 add = add + jnp.where(lanes == C - 1, high_col[:, at:at + 1], 0.0)
                 add = add + jnp.where(rows == 0, row_r[n, 0, at:at + 1], 0.0)
                 add = add + jnp.where(rows == R - 1, row_r[n, 1, at:at + 1], 0.0)
-                base[c, l] += weight * add
+                target[c, l] = base[c, l] + weight * add
 
     def field(n):
         edge = join([d_r[n, j, L] for j in range(nby)], 0)
@@ -718,22 +731,23 @@
             phi = phis[l]
             low = d_r[n, 0, L + 1, l:l + 1]
             high = d_r[n, nby - 1, L + 1, l:l + 1]
-            along_x = -0.5 * (x_next(phi, high) - x_prev(phi, low))
-            along_y = -0.5 * (y_next(phi, edge[:, L + l:L + l + 1])
-                              - y_prev(phi, edge[:, l:l + 1]))
+            along_x = 0.5 * (x_next(phi, high) - x_prev(phi, low))
+            along_y = 0.5 * (y_next(phi, edge[:, L + l:L + l + 1])
+                             - y_prev(phi, edge[:, l:l + 1]))
             above = phis[l + 1] if l + 1 < L else zero
             below = phis[l - 1] if l else zero
-            yield l, (along_x, along_y, -0.5 * (above - below))
-
+            yield l, (along_x, along_y, 0.5 * (above - below))
+
+    loads[0].wait()
     charge(0, p_in)
     flank_start(0, p_in)
     pl.semaphore_wait(barrier, len(others))
     first_a = among_y(a_s, a_r, 0)
     flanks = flank_send(0)
-    loads[0].wait()
+    loads[1].wait()
     relax_inside(p_in)
-    loads[1].wait()
     loads[2].wait()
+    loads[3].wait()
     wave_x = wx[0:1]
     wave_y = join([wy[...]] * (NX // C), 1)
     lateral = wave_x + wave_y
@@ -746,13 +760,13 @@
         coef[l] = inverse
         previous = inter[l + 1] * inverse
         ratio[l] = previous
-    loads[3].wait()
     loads[4].wait()
+    loads[5].wait()
     wait(first_a)
     y_forward(0)
     first_b = spread(b_s, b_r, 0, False)
     wait(flanks)
-    relax_edges(0)
+    relax_edges(0, base)
     charge(1, base)
     second_a = among_y(a_s, a_r, 1)
     wait(second_a)
@@ -780,23 +794,22 @@
     wait(first_c)
     y_backward(0)
     first_d = among_y(d_s, d_r, 0)
+    wait(second_c)
+    y_backward(1)
+    second_d = among_y(d_s, d_r, 1)
     wait(first_d)
     for l, parts in field(0):
         for c in range(3):
-            p_mid[c, l] = base[c, l] + step_size * parts[c]
+            p_mid[c, l] = base[c, l] - step_size * parts[c]
     flank_start(1, p_mid)
     flanks = flank_send(1)
-    wait(second_c)
-    y_backward(1)
-    second_d = among_y(d_s, d_r, 1)
     relax_inside(p_mid)
     wait(flanks)
-    relax_edges(1)
+    relax_edges(1, base_o)
     wait(second_d)
     for l, parts in field(1):
         for c in range(3):
-            f_out[c, l] = parts[c]
-            p_out[c, l] = base[c, l] + step_size * parts[c]
+            down_o[c, l] = parts[c]
     for send in sends:
         send()
 
@@ -819,7 +832,6 @@
     wave_y = 4.0 * np.sin(np.pi * mode / grid_y) ** 2
     wave_y = jnp.asarray(np.tile(wave_y[:, None], (1, C)).astype(np.float32))
     f32 = jnp.float32
-    vmem = pl.BlockSpec(memory_space=pltpu.VMEM)
     hbm = pl.BlockSpec(memory_space=pltpu.HBM)
     smem = pl.BlockSpec(memory_space=pltpu.SMEM)
     S = 2
@@ -834,21 +846,23 @@
         pltpu.VMEM((S, 2, 3 * L, C), f32), pltpu.VMEM((S, 2, 3 * L, C), f32),
         pltpu.VMEM((S, R, C), f32), pltpu.VMEM((S, 2, R, C), f32),
         pltpu.SemaphoreType.DMA((n_copies,)), pltpu.SemaphoreType.DMA((n_copies,)),
+        pltpu.VMEM((3, L, R, C), f32),
         pltpu.VMEM((L, R, C), f32), pltpu.VMEM(wave_x.shape, f32), pltpu.VMEM((per, C), f32),
         pltpu.VMEM(hx.shape, hx.dtype), pltpu.VMEM(hy.shape, hy.dtype),
-        pltpu.SemaphoreType.DMA((5,)),
+        pltpu.SemaphoreType.DMA((6,)),
     ]
-    out = jax.ShapeDtypeStruct(polarization.shape, f32)
-    return pl.pallas_call(
+    out = pltpu.VMEM(polarization.shape, f32)
+    base, down = pl.pallas_call(
         functools.partial(fused, (L, R, C, nbx, nby)),
         out_shape=(out, out),
-        in_specs=[vmem, hbm, smem, smem, smem, smem, hbm, hbm, hbm, hbm],
-        out_specs=(vmem, vmem),
+        in_specs=[hbm, hbm, smem, smem, smem, smem, hbm, hbm, hbm, hbm],
+        out_specs=(pl.BlockSpec(memory_space=pltpu.VMEM), pl.BlockSpec(memory_space=pltpu.VMEM)),
         scratch_shapes=scratch,
         compiler_params=pltpu.CompilerParams(
-            collective_id=0, has_side_effects=True, vmem_limit_bytes=60 * 1000 * 1000),
+            collective_id=0, has_side_effects=True, vmem_limit_bytes=66 * 1000 * 1000),
     )(polarization, alpha_field, landau, stiffness, permittivity, interfaces,
       wave_x, wave_y, hx, hy)
+    return base - step_size * down, -down
 
 
 def solution(mesh):

time: 43.6 us -> 40.5 us (0.929)
  local copies, waits for them, and re-layouts: 2.57 us -> 0 us
  Pallas kernels: 40.2 us -> 38.8 us
  other arithmetic: 0 us -> 0.96 us
    unnamed x4 -> x0, local copies, waits for them, and re-layouts: 2.57 us -> none
    pallas_call x1, Pallas kernels: 40.2 us -> 38.8 us  [fused_shards(): pl.pallas_call(functools.partial(fused, (L, R, C, nbx, nby)), out_shape=(...]
    neg x0 -> x1, other arithmetic: none -> 0.96 us  [fused_shards(): return (base - step_size * down, -down)]
where the time goes in v2:
time: 40.5 us; the launch traced here: 40.4 us
  Pallas kernels  38.8 us (96%)
  other arithmetic  0.96 us (2%)
  between operations  0.64 us (2%)
    pallas_call x1, Pallas kernels, fused_shards(): pl.pallas_call(functools.partial(fused, (L, R, C, nbx, nby)), out_shape=(...  38.8 us
    neg x1, other arithmetic, fused_shards(): return (base - step_size * down, -down)  0.96 us

profile of v2, /device:TPU:0, one launch (start us, length us, event | category | flops | bytes accessed | tf_op | source)
XLA Modules:
  0.0 40.4 jit_solution(13304035594921854606)
XLA Ops:
  0.6 38.8 %shard_map.113 = (f32[3,8,32,128]{3,2,1,0:T(8,128)S(1)}, f32[3,8,32,128]{3,2,1,0:T(8,128)S(1)}) custom-call(f32[3,8,32,128]{3,2,1,0:T(8,128)} %p_h.1, f32[8,32,128]{2,1,0:T(8,128)} %alpha_h.1, f32[3,8]{1,0:T(4,128)} %landau.1, f32[8]{0:T(128)} %stiff.1, f32[8]{0:T(128)} %perm.1, f32[9]{0:T(128)} %inter.1, f32[8,256]{1,0:T(8,128)} %constant.12.clone.wx_h, ...), custom_call_target="tpu_custom_call" | custom-call | tf_op jit(solution)/shard_map/pallas_call | solution.py:855
  39.4 1.0 %fusion = (f32[3,8,32,128]{3,2,1,0:T(8,128)}, f32[3,8,32,128]{3,2,1,0:T(8,128)}) fusion(f32[3,8,32,128]{3,2,1,0:T(8,128)S(1)} %get-tuple-element.5, f32[3,8,32,128]{3,2,1,0:T(8,128)S(1)} %get-tuple-element.4), kind=kLoop, calls=%fused_computation.1 | loop fusion | flops 294912 | bytes 1572864 | tf_op jit(solution)/shard_map/neg | solution.py:865

commit v3 on v2

--- a/solution.py
+++ b/solution.py
@@ -423,7 +423,7 @@
 def fits(L, R, C, nbx, nby):
     slab = R // nby
     return (L == nbx and slab == 8 and slab * nby == R and nby > 1 and C % L == 0
-            and nbx & (nbx - 1) == 0 and nby & (nby - 1) == 0)
+            and nbx > 2 and nbx & (nbx - 1) == 0 and nby & (nby - 1) == 0)
 
 
 def partner(index, mask, size):
@@ -444,11 +444,10 @@
           base_o, down_o, *scratch):
     L, R, C, nbx, nby = sizes
     (p_mid, base, coef, ratio, a_s, a_r, b_s, b_r, c_s, c_r, d_s, d_r,
-     row_s, row_r, col_s, col_r, ssem, rsem, p_in, alpha, wx, wy, hx, hy, local_sem) = scratch
+     row_s, row_r, col_s, col_r, ssem, rsem, known, p_in, alpha, wx, wy, hx, hy, local_sem) = scratch
     slab = R // nby
     per = C // L
     NX, NY = nbx * R, nby * C
-    thick = slab + 1
     bx = lax.axis_index("bx")
     by = lax.axis_index("by")
     scale = 1.0 / (NX * NY)
@@ -462,7 +461,9 @@
     at_y = [partner(by, b, nby) for b in range(nby)]
     others = [(a, b) for b in range(nby) for a in range(nbx) if a or b]
     others.sort(key=lambda ab: -(ab[0] // 2 + ab[0] % 2 + ab[1] // 2))
-    for a, b in others:
+    reach = [1 << i for i in range(1, nbx.bit_length() - 1)]
+    greeted = [(a, b) for a, b in others if a < 2] + [(a, 0) for a in reach]
+    for a, b in greeted:
         pl.semaphore_signal(
             barrier, inc=1, device_id={"bx": at_x[a], "by": at_y[b]}, device_id_type=MESH)
     mine = pl.multiple_of((bx * nby + by) * per, per)
@@ -501,38 +502,90 @@
     def y_prev(f, low):
         return jnp.where(lanes == 0, low, pltpu.roll(f, 1, 1))
 
-    def charge(n, src):
+    def charge(n, src, ring):
+        sides = (0, nby - 1)
         edge = zero
         for l in range(L):
             along_x, along_y = src[0, l], src[1, l]
             above = src[2, l + 1] if l + 1 < L else zero
             below = src[2, l - 1] if l else zero
-            value = -0.5 * ((x_next(along_x, 0.0) - x_prev(along_x, 0.0))
-                            + (y_next(along_y, 0.0) - y_prev(along_y, 0.0)) + (above - below))
+            low = high = left = right = 0.0
+            if ring:
+                lines, column = ring
+                low, high = lines[0][0][l:l + 1], lines[1][0][l:l + 1]
+                left = column[:, L + l:L + l + 1]
+                right = column[:, C // 2 + L + l:C // 2 + L + l + 1]
+            value = -0.5 * ((x_next(along_x, high) - x_prev(along_x, low))
+                            + (y_next(along_y, right) - y_prev(along_y, left)) + (above - below))
             for j in range(nby):
                 a_s[n, j, l] = value[j * slab:(j + 1) * slab]
-            a_s[n, 0, L + 1, l:l + 1] = -0.5 * along_x[0:1]
-            a_s[n, nby - 1, L + 1, l:l + 1] = 0.5 * along_x[R - 1:R]
             edge = jnp.where(lanes == l, -0.5 * along_y[:, 0:1], edge)
             edge = jnp.where(lanes == L + l, 0.5 * along_y[:, C - 1:C], edge)
+        near = [-0.5 * join([src[0, l, 0:1] for l in range(L)], 0),
+                0.5 * join([src[0, l, R - 1:R] for l in range(L)], 0)]
+        corner = [None, None]
+        if ring:
+            for side, sign in enumerate((-0.5, 0.5)):
+                first, second, third = lines[side]
+                turned = (jnp.where(lanes8 == C - 1, 0.0, pltpu.roll(second, C - 1, 1))
+                          - jnp.where(lanes8 == 0, 0.0, pltpu.roll(second, 1, 1)))
+                risen = (jnp.where(rows8 == L - 1, 0.0, pltpu.roll(third, L - 1, 0))
+                         - jnp.where(rows8 == 0, 0.0, pltpu.roll(third, 1, 0)))
+                near[side] = near[side] - 0.5 * (turned + risen)
+                a_s[n, sides[side], L + 2] = sign * first
+                corner[side] = jnp.where(
+                    lanes8 == 4 * L, sign * first[:, 0:1] - 0.5 * second[:, 0:1],
+                    jnp.where(lanes8 == 4 * L + 1,
+                              sign * first[:, C - 1:C] + 0.5 * second[:, C - 1:C], 0.0))
+            layer = lanes % L
+            turned = -0.5 * (x_next(column, 0.0) - x_prev(column, 0.0))
+            risen = -0.5 * (jnp.where(layer == L - 1, 0.0, pltpu.roll(column, C - 1, 1))
+                            - jnp.where(layer == 0, 0.0, pltpu.roll(column, 1, 1)))
+            both = turned + pltpu.roll(risen, C - 2 * L, 1)
+            low = edge + both
+            high = edge + pltpu.roll(both, C // 2 + L, 1)
+            far_low = -0.5 * pltpu.roll(column, L, 1)
+            far_high = 0.5 * pltpu.roll(column, C // 2 + 2 * L, 1)
+            group = lanes // L
+            edge = jnp.where(group == 0, low, jnp.where(group == 1, high, jnp.where(
+                group == 2, far_low, jnp.where(group == 3, far_high, 0.0))))
+        for side in range(2):
+            a_s[n, sides[side], L + 1] = near[side]
         for j in range(nby):
-            a_s[n, j, L] = edge[j * slab:(j + 1) * slab]
-            if 0 < j < nby - 1:
+            piece = edge[j * slab:(j + 1) * slab]
+            if ring and j in sides:
+                piece = piece + corner[sides.index(j)]
+            a_s[n, j, L] = piece
+            if j not in sides:
                 a_s[n, j, L + 1] = jnp.zeros((L, C), f32)
-
-    def among_y(source, landing, n):
+                if ring:
+                    a_s[n, j, L + 2] = jnp.zeros((L, C), f32)
+
+    def ring_of(n):
+        weight8 = zero8
+        weight = zero
+        layer = lanes % L
+        for l in range(L):
+            weight8 = jnp.where(rows8 == l, step_size * stiff[l], weight8)
+            weight = jnp.where(layer == l, step_size * stiff[l], weight)
+        lines = [[weight8 * row_s[n, side, c * L:(c + 1) * L] for c in range(3)]
+                 for side in range(2)]
+        return lines, weight * col_s[n]
+
+    def among_y(source, landing, n, count):
+        part = pl.ds(0, count)
         copies = []
         for b in range(nby - 1, 0, -1):
             to = at_y[b]
-            copies.append(push(source.at[n, to], landing.at[n, by], {"by": to}))
-        landing[n, by] = source[n, by]
+            copies.append(push(source.at[n, to, part], landing.at[n, by, part], {"by": to}))
+        landing[n, by, 0:count] = source[n, by, 0:count]
         return copies
 
     def wait(copies):
         for copy in copies:
             copy.wait_recv()
 
-    def spread(source, landing, n, flip):
+    def spread(source, landing, n, flip, thick):
         part = pl.ds(0, thick)
         copies = []
         for a, b in others:
@@ -593,22 +646,34 @@
                 extra = jnp.where(
                     lanes8 == 0, from_left[:, L + l:L + l + 1],
                     jnp.where(lanes8 == C - 1, from_right[:, l:l + 1], 0.0))
+                if n:
+                    extra = jnp.where(
+                        lanes8 == 1, from_left[:, 3 * L + l:3 * L + l + 1],
+                        jnp.where(lanes8 == C - 2, from_right[:, 2 * L + l:2 * L + l + 1], extra))
                 tiles.append(a_r[n, j, l] + extra)
-            columns.append(join(tiles + [a_r[n, j, L + 1], zero8], 0))
+            near, far = a_r[n, j, L + 1], zero8
+            if n:
+                near = near + jnp.where(
+                    lanes8 == 0, from_left[:, 4 * L + 1:4 * L + 2],
+                    jnp.where(lanes8 == C - 1, from_right[:, 4 * L:4 * L + 1], 0.0))
+                far = a_r[n, j, L + 2]
+            columns.append(join(tiles + [near, far], 0))
         out = y_table(join(columns, 1))
         tiles = [join([out[l * slab:(l + 1) * slab, t * C:(t + 1) * C] for t in range(nby)], 0)
                  for l in range(L)]
         tiles = swap_groups(tiles)
         for t in range(nby):
-            halo = swap_rows(out[L * slab:L * slab + L, t * C:(t + 1) * C])
+            halos = [swap_rows(out[(L + k) * slab:(L + k) * slab + L, t * C:(t + 1) * C])
+                     for k in range(1 + n)]
             for e in range(L):
                 b_s[n, t, e, 0:slab] = tiles[e][t * slab:(t + 1) * slab]
-                b_s[n, t, e, slab:thick] = halo[e:e + 1]
+                for k, halo in enumerate(halos):
+                    b_s[n, t, e, slab + k:slab + k + 1] = halo[e:e + 1]
 
     def y_backward(n):
         tiles = swap_groups([join([c_r[n, t, e, 0:slab] for t in range(nby)], 0)
                              for e in range(L)])
-        halos = [swap_rows(join([c_r[n, t, e, slab:thick] for e in range(L)], 0))
+        halos = [swap_rows(join([c_r[n, t, e, slab:slab + 1] for e in range(L)], 0))
                  for t in range(nby)]
         lines = [join([tiles[l][t * slab:(t + 1) * slab] for t in range(nby)], 1)
                  for l in range(L)]
@@ -630,12 +695,14 @@
         for i in range(nbx):
             for j in range(nby):
                 tile = b_r[n, i, j, 0:slab]
-                if j == 0:
-                    tile = tile + jnp.where(
-                        rows8 == 0, b_r[n, (i + nbx - 1) % nbx, nby - 1, slab:thick], 0.0)
-                if j == nby - 1:
-                    tile = tile + jnp.where(
-                        rows8 == slab - 1, b_r[n, (i + 1) % nbx, 0, slab:thick], 0.0)
+                for k in range(1 + n):
+                    line = slice(slab + k, slab + k + 1)
+                    if j == 0:
+                        tile = tile + jnp.where(
+                            rows8 == k, b_r[n, (i + nbx - 1) % nbx, nby - 1, line], 0.0)
+                    if j == nby - 1:
+                        tile = tile + jnp.where(
+                            rows8 == slab - 1 - k, b_r[n, (i + 1) % nbx, 0, line], 0.0)
                 tiles.append(tile)
         full = join(tiles, 0).T
         high = full.astype(jnp.bfloat16)
@@ -672,7 +739,7 @@
                     line = (at + NX - 1) % NX
                 else:
                     line = (at + slab) % NX
-                c_s[n, i, j, slab:thick] = out[line:line + 1]
+                c_s[n, i, j, slab:slab + 1] = out[line:line + 1]
 
     def flank_start(n, src):
         tile = zero
@@ -739,13 +806,23 @@
             yield l, (along_x, along_y, 0.5 * (above - below))
 
     loads[0].wait()
-    charge(0, p_in)
+    charge(0, p_in, None)
     flank_start(0, p_in)
-    pl.semaphore_wait(barrier, len(others))
-    first_a = among_y(a_s, a_r, 0)
-    flanks = flank_send(0)
     loads[1].wait()
     relax_inside(p_in)
+    charge(1, base, ring_of(0))
+    pl.semaphore_wait(barrier, len(greeted))
+
+    def tell(at):
+        pl.semaphore_signal(
+            known.at[at], inc=1, device_id={"bx": at_x[reach[at]]}, device_id_type=MESH)
+
+    tell(0)
+    first_a = among_y(a_s, a_r, 0, L + 2)
+    second_a = among_y(a_s, a_r, 1, L + 3)
+    for at in range(1, len(reach)):
+        pl.semaphore_wait(known.at[at - 1], 1)
+        tell(at)
     loads[2].wait()
     loads[3].wait()
     wave_x = wx[0:1]
@@ -764,18 +841,18 @@
     loads[5].wait()
     wait(first_a)
     y_forward(0)
-    first_b = spread(b_s, b_r, 0, False)
-    wait(flanks)
-    relax_edges(0, base)
-    charge(1, base)
-    second_a = among_y(a_s, a_r, 1)
+    pl.semaphore_wait(known.at[len(reach) - 1], 1)
+    first_b = spread(b_s, b_r, 0, False, slab + 1)
     wait(second_a)
     y_forward(1)
-    second_b = spread(b_s, b_r, 1, False)
+    second_b = spread(b_s, b_r, 1, False, slab + 2)
+    flanks = flank_send(0)
     wait(first_b)
     values = solve(spectrum(0))
     x_backward(0, values)
-    first_c = spread(c_s, c_r, 0, True)
+    first_c = spread(c_s, c_r, 0, True, slab + 1)
+    wait(flanks)
+    relax_edges(0, base)
     bend = -(wave_x * (1.0 - 0.25 * wave_x) + wave_y * (1.0 - 0.25 * wave_y))
     slopes = []
     none = jnp.zeros_like(values[0])
@@ -790,13 +867,13 @@
         moved.append(step_size * (bend * values[l] + 0.5 * (above - below)))
     wait(second_b)
     x_backward(1, solve([here + more for here, more in zip(spectrum(1), moved)]))
-    second_c = spread(c_s, c_r, 1, True)
+    second_c = spread(c_s, c_r, 1, True, slab + 1)
     wait(first_c)
     y_backward(0)
-    first_d = among_y(d_s, d_r, 0)
+    first_d = among_y(d_s, d_r, 0, L + 2)
     wait(second_c)
     y_backward(1)
-    second_d = among_y(d_s, d_r, 1)
+    second_d = among_y(d_s, d_r, 1, L + 2)
     wait(first_d)
     for l, parts in field(0):
         for c in range(3):
@@ -836,7 +913,7 @@
     smem = pl.BlockSpec(memory_space=pltpu.SMEM)
     S = 2
     n_copies = S * (4 + 2 * (nby - 1) + 2 * (nbx * nby - 1))
-    by_y = pltpu.VMEM((S, nby, L + 2, 8, C), f32)
+    by_y = pltpu.VMEM((S, nby, L + 3, 8, C), f32)
     by_mode = pltpu.VMEM((S, nby, nbx, 16, C), f32)
     by_place = pltpu.VMEM((S, nbx, nby, 16, C), f32)
     scratch = [
@@ -846,7 +923,7 @@
         pltpu.VMEM((S, 2, 3 * L, C), f32), pltpu.VMEM((S, 2, 3 * L, C), f32),
         pltpu.VMEM((S, R, C), f32), pltpu.VMEM((S, 2, R, C), f32),
         pltpu.SemaphoreType.DMA((n_copies,)), pltpu.SemaphoreType.DMA((n_copies,)),
-        pltpu.VMEM((3, L, R, C), f32),
+        pltpu.SemaphoreType.REGULAR((nbx.bit_length(),)), pltpu.VMEM((3, L, R, C), f32),
         pltpu.VMEM((L, R, C), f32), pltpu.VMEM(wave_x.shape, f32), pltpu.VMEM((per, C), f32),
         pltpu.VMEM(hx.shape, hx.dtype), pltpu.VMEM(hy.shape, hy.dtype),
         pltpu.SemaphoreType.DMA((6,)),

time: 40.5 us -> 38.2 us (0.943)
  Pallas kernels: 38.8 us -> 36.5 us
    pallas_call x1, Pallas kernels: 38.8 us -> 36.5 us  [fused_shards(): pl.pallas_call(functools.partial(fused, (L, R, C, nbx, nby)), out_shape=(...]
where the time goes in v3:
time: 38.2 us; the launch traced here: 38.1 us
  Pallas kernels  36.5 us (96%)
  other arithmetic  0.96 us (3%)
  between operations  0.64 us (2%)
    pallas_call x1, Pallas kernels, fused_shards(): pl.pallas_call(functools.partial(fused, (L, R, C, nbx, nby)), out_shape=(...  36.5 us
    neg x1, other arithmetic, fused_shards(): return (base - step_size * down, -down)  0.96 us

profile of v3, /device:TPU:0, one launch (start us, length us, event | category | flops | bytes accessed | tf_op | source)
XLA Modules:
  0.0 38.1 jit_solution(14899224843282360310)
XLA Ops:
  0.6 36.5 %shard_map.113 = (f32[3,8,32,128]{3,2,1,0:T(8,128)S(1)}, f32[3,8,32,128]{3,2,1,0:T(8,128)S(1)}) custom-call(f32[3,8,32,128]{3,2,1,0:T(8,128)} %p_h.1, f32[8,32,128]{2,1,0:T(8,128)} %alpha_h.1, f32[3,8]{1,0:T(4,128)} %landau.1, f32[8]{0:T(128)} %stiff.1, f32[8]{0:T(128)} %perm.1, f32[9]{0:T(128)} %inter.1, f32[8,256]{1,0:T(8,128)} %constant.12.clone.wx_h, ...), custom_call_target="tpu_custom_call" | custom-call | tf_op jit(solution)/shard_map/pallas_call | solution.py:932
  37.1 1.0 %fusion = (f32[3,8,32,128]{3,2,1,0:T(8,128)}, f32[3,8,32,128]{3,2,1,0:T(8,128)}) fusion(f32[3,8,32,128]{3,2,1,0:T(8,128)S(1)} %get-tuple-element.5, f32[3,8,32,128]{3,2,1,0:T(8,128)S(1)} %get-tuple-element.4), kind=kLoop, calls=%fused_computation.1 | loop fusion | flops 294912 | bytes 1572864 | tf_op jit(solution)/shard_map/neg | solution.py:942

commit v4 on v3

--- a/solution.py
+++ b/solution.py
@@ -422,7 +422,7 @@
 
 def fits(L, R, C, nbx, nby):
     slab = R // nby
-    return (L == nbx and slab == 8 and slab * nby == R and nby > 1 and C % L == 0
+    return (L == nbx and slab == 8 and slab * nby == R and nby > 1 and C % (8 * L) == 0
             and nbx > 2 and nbx & (nbx - 1) == 0 and nby & (nby - 1) == 0)
 
 
@@ -673,22 +673,33 @@
     def y_backward(n):
         tiles = swap_groups([join([c_r[n, t, e, 0:slab] for t in range(nby)], 0)
                              for e in range(L)])
-        halos = [swap_rows(join([c_r[n, t, e, slab:slab + 1] for e in range(L)], 0))
-                 for t in range(nby)]
+        rims = [join([swap_rows(join([c_r[n, t, e, slab + k:slab + k + 1] for e in range(L)], 0))
+                      for t in range(nby)], 1) for k in range(2 - n)]
+        if n:
+            rims.append(jnp.zeros((slab, NY), f32))
         lines = [join([tiles[l][t * slab:(t + 1) * slab] for t in range(nby)], 1)
                  for l in range(L)]
-        lines += [join(halos, 1), jnp.zeros((slab, NY), f32)]
-        out = y_table(join(lines, 0))
+        out = y_table(join(lines + rims, 0))
+        near = out[L * slab:L * slab + L]
         for j in range(nby):
             edge = zero8
-            left, right = (j + nby - 1) % nby, (j + 1) % nby
+            left, right = (j + nby - 1) % nby * C, (j + 1) % nby * C
+            wanted = [left + C - 1, right]
+            if n == 0:
+                wanted += [left + C - 2, right + 1, None, j * C, j * C + C - 1]
+                edge = jnp.where(lanes8 == 4 * L, near[:, left + C - 1:left + C],
+                                 jnp.where(lanes8 == 4 * L + 1, near[:, right:right + 1], edge))
             for l in range(L):
                 line = out[l * slab:(l + 1) * slab]
                 d_s[n, j, l] = line[:, j * C:(j + 1) * C]
-                edge = jnp.where(lanes8 == l, line[:, left * C + C - 1:left * C + C], edge)
-                edge = jnp.where(lanes8 == L + l, line[:, right * C:right * C + 1], edge)
+                for at, column in enumerate(wanted):
+                    if column is not None:
+                        edge = jnp.where(
+                            lanes8 == at * L + l, line[:, column:column + 1], edge)
             d_s[n, j, L] = edge
-            d_s[n, j, L + 1] = out[L * slab:L * slab + L, j * C:(j + 1) * C]
+            for k in range(2 - n):
+                d_s[n, j, L + 1 + k] = out[(L + k) * slab:(L + k) * slab + L,
+                                           j * C:(j + 1) * C]
 
     def spectrum(n):
         tiles = []
@@ -735,11 +746,9 @@
             for j in range(nby):
                 at = i * R + j * slab
                 c_s[n, i, j, 0:slab] = out[at:at + slab]
-                if j == 0:
-                    line = (at + NX - 1) % NX
-                else:
-                    line = (at + slab) % NX
-                c_s[n, i, j, slab:slab + 1] = out[line:line + 1]
+                for k in range(2 - n):
+                    line = (at - 1 - k if j == 0 else at + slab + k) % NX
+                    c_s[n, i, j, slab + k:slab + k + 1] = out[line:line + 1]
 
     def flank_start(n, src):
         tile = zero
@@ -778,18 +787,54 @@
                     + 6.0 * landau[2, l] * (square * square))
                 base[c, l] = cell - step_size * (drive - smooth)
 
-    def relax_edges(n, target):
-        low_col = col_r[n, 0]
-        high_col = col_r[n, 1]
+    def flank_lines(n):
+        return [[row_r[n, side, c * L:(c + 1) * L] for c in range(3)] for side in range(2)]
+
+    def relax_edges(lines, low_col, high_col, target):
         for l in range(L):
             weight = step_size * stiff[l]
             for c in range(3):
                 at = c * L + l
                 add = jnp.where(lanes == 0, low_col[:, C // 2 + at:C // 2 + at + 1], 0.0)
                 add = add + jnp.where(lanes == C - 1, high_col[:, at:at + 1], 0.0)
-                add = add + jnp.where(rows == 0, row_r[n, 0, at:at + 1], 0.0)
-                add = add + jnp.where(rows == R - 1, row_r[n, 1, at:at + 1], 0.0)
+                add = add + jnp.where(rows == 0, lines[0][c][l:l + 1], 0.0)
+                add = add + jnp.where(rows == R - 1, lines[1][c][l:l + 1], 0.0)
                 target[c, l] = base[c, l] + weight * add
+
+    def moved_rim():
+        lines = flank_lines(1)
+        corners = []
+        for side, owner in enumerate((0, nby - 1)):
+            inner = join([d_r[0, owner, l, side * (slab - 1):side * (slab - 1) + 1]
+                          for l in range(L)], 0)
+            near, far = d_r[0, owner, L + 1], d_r[0, owner, L + 2]
+            edge = d_r[0, owner, L]
+            low, high = edge[:, 4 * L:4 * L + 1], edge[:, 4 * L + 1:4 * L + 2]
+            down = [inner - far if side == 0 else far - inner,
+                    jnp.where(lanes8 == C - 1, high, pltpu.roll(near, C - 1, 1))
+                    - jnp.where(lanes8 == 0, low, pltpu.roll(near, 1, 1)),
+                    jnp.where(rows8 == L - 1, 0.0, pltpu.roll(near, L - 1, 0))
+                    - jnp.where(rows8 == 0, 0.0, pltpu.roll(near, 1, 0))]
+            lines[side] = [line - (0.5 * step_size) * part
+                           for line, part in zip(lines[side], down)]
+            spot = jnp.where(lanes8 == rows8, low, jnp.where(lanes8 == rows8 + L, high, 0.0))
+            corners.append(jnp.sum(spot, axis=0, keepdims=True))
+        edge = join([d_r[0, j, L] for j in range(nby)], 0)
+        layer = lanes % L
+        group = lanes // L
+        across = pltpu.roll(edge, C - 5 * L, 1) - pltpu.roll(edge, C - 2 * L, 1)
+        down = [x_next(edge, corners[1]) - x_prev(edge, corners[0]),
+                jnp.where(group == 0, across, -across),
+                jnp.where(layer == L - 1, 0.0, pltpu.roll(edge, C - 1, 1))
+                - jnp.where(layer == 0, 0.0, pltpu.roll(edge, 1, 1))]
+        low_col, high_col = col_r[1, 0], col_r[1, 1]
+        for c in range(3):
+            part = (0.5 * step_size) * down[c]
+            low_col = low_col - jnp.where(
+                group == C // (2 * L) + c, pltpu.roll(part, C // 2 + c * L, 1), 0.0)
+            high_col = high_col - jnp.where(
+                group == c, pltpu.roll(part, (C + c * L - L) % C, 1), 0.0)
+        return lines, low_col, high_col
 
     def field(n):
         edge = join([d_r[n, j, L] for j in range(nby)], 0)
@@ -850,9 +895,7 @@
     wait(first_b)
     values = solve(spectrum(0))
     x_backward(0, values)
-    first_c = spread(c_s, c_r, 0, True, slab + 1)
-    wait(flanks)
-    relax_edges(0, base)
+    first_c = spread(c_s, c_r, 0, True, slab + 2)
     bend = -(wave_x * (1.0 - 0.25 * wave_x) + wave_y * (1.0 - 0.25 * wave_y))
     slopes = []
     none = jnp.zeros_like(values[0])
@@ -868,9 +911,13 @@
     wait(second_b)
     x_backward(1, solve([here + more for here, more in zip(spectrum(1), moved)]))
     second_c = spread(c_s, c_r, 1, True, slab + 1)
+    wait(flanks)
+    relax_edges(flank_lines(0), col_r[0, 0], col_r[0, 1], base)
+    flank_start(1, base)
+    flanks = flank_send(1)
     wait(first_c)
     y_backward(0)
-    first_d = among_y(d_s, d_r, 0, L + 2)
+    first_d = among_y(d_s, d_r, 0, L + 3)
     wait(second_c)
     y_backward(1)
     second_d = among_y(d_s, d_r, 1, L + 2)
@@ -878,11 +925,10 @@
     for l, parts in field(0):
         for c in range(3):
             p_mid[c, l] = base[c, l] - step_size * parts[c]
-    flank_start(1, p_mid)
-    flanks = flank_send(1)
+    wait(flanks)
+    rim = moved_rim()
     relax_inside(p_mid)
-    wait(flanks)
-    relax_edges(1, base_o)
+    relax_edges(*rim, base_o)
     wait(second_d)
     for l, parts in field(1):
         for c in range(3):

time: 38.2 us -> 36.8 us (0.963)
  Pallas kernels: 36.5 us -> 35.1 us
    pallas_call x1, Pallas kernels: 36.5 us -> 35.1 us  [fused_shards(): pl.pallas_call(functools.partial(fused, (L, R, C, nbx, nby)), out_shape=(...]
where the time goes in v4:
time: 36.8 us; the launch traced here: 36.7 us
  Pallas kernels  35.1 us (95%)
  other arithmetic  0.96 us (3%)
  between operations  0.64 us (2%)
    pallas_call x1, Pallas kernels, fused_shards(): pl.pallas_call(functools.partial(fused, (L, R, C, nbx, nby)), out_shape=(...  35.1 us
    neg x1, other arithmetic, fused_shards(): return (base - step_size * down, -down)  0.96 us

profile of v4, /device:TPU:0, one launch (start us, length us, event | category | flops | bytes accessed | tf_op | source)
XLA Modules:
  0.0 36.7 jit_solution(7665412999759439764)
XLA Ops:
  0.6 35.1 %shard_map.113 = (f32[3,8,32,128]{3,2,1,0:T(8,128)S(1)}, f32[3,8,32,128]{3,2,1,0:T(8,128)S(1)}) custom-call(f32[3,8,32,128]{3,2,1,0:T(8,128)} %p_h.1, f32[8,32,128]{2,1,0:T(8,128)} %alpha_h.1, f32[3,8]{1,0:T(4,128)} %landau.1, f32[8]{0:T(128)} %stiff.1, f32[8]{0:T(128)} %perm.1, f32[9]{0:T(128)} %inter.1, f32[8,256]{1,0:T(8,128)} %constant.12.clone.wx_h, ...), custom_call_target="tpu_custom_call" | custom-call | tf_op jit(solution)/shard_map/pallas_call | solution.py:978
  35.7 1.0 %fusion = (f32[3,8,32,128]{3,2,1,0:T(8,128)}, f32[3,8,32,128]{3,2,1,0:T(8,128)}) fusion(f32[3,8,32,128]{3,2,1,0:T(8,128)S(1)} %get-tuple-element.5, f32[3,8,32,128]{3,2,1,0:T(8,128)S(1)} %get-tuple-element.4), kind=kLoop, calls=%fused_computation.1 | loop fusion | flops 294912 | bytes 1572864 | tf_op jit(solution)/shard_map/neg | solution.py:988

commit v5 on v4

--- a/solution.py
+++ b/solution.py
@@ -557,9 +557,7 @@
                 piece = piece + corner[sides.index(j)]
             a_s[n, j, L] = piece
             if j not in sides:
-                a_s[n, j, L + 1] = jnp.zeros((L, C), f32)
-                if ring:
-                    a_s[n, j, L + 2] = jnp.zeros((L, C), f32)
+                a_s[n, j, L + 1:L + 3] = jnp.zeros((2, slab, C), f32)
 
     def ring_of(n):
         weight8 = zero8
@@ -572,34 +570,87 @@
                  for side in range(2)]
         return lines, weight * col_s[n]
 
-    def among_y(source, landing, n, count):
-        part = pl.ds(0, count)
-        copies = []
-        for b in range(nby - 1, 0, -1):
-            to = at_y[b]
-            copies.append(push(source.at[n, to, part], landing.at[n, by, part], {"by": to}))
+    rim_slab = (by == 0) | (by == nby - 1)
+
+    def has_rim(b, here):
+        return nby != 4 or (b in (0, nby - 1)) == here
+
+    def either(action):
+        if nby != 4:
+            action(True)
+        else:
+            pl.when(rim_slab)(functools.partial(action, True))
+            pl.when(jnp.logical_not(rim_slab))(functools.partial(action, False))
+
+    def exchange(targets, build, by_target):
+        first = slots[0]
+        slots[0] += len(targets)
+
+        def make(at, whole):
+            a, b = targets[at]
+            src, dst = build(a, b, whole)
+            return pltpu.make_async_remote_copy(
+                src_ref=src, dst_ref=dst, send_sem=ssem.at[first + at],
+                recv_sem=rsem.at[first + at], device_id={"bx": at_x[a], "by": at_y[b]},
+                device_id_type=MESH)
+
+        def outgoing(here):
+            return [make(at, has_rim(b, here) if by_target else here)
+                    for at, (a, b) in enumerate(targets)]
+
+        def start(here):
+            for copy in outgoing(here):
+                copy.start()
+
+        def sent(here):
+            for copy in outgoing(here):
+                copy.wait_send()
+
+        def came(here):
+            for at, (a, b) in enumerate(targets):
+                make(at, here if by_target else has_rim(b, here)).wait_recv()
+
+        either(start)
+        sends.append(functools.partial(either, sent))
+        return functools.partial(either, came)
+
+    def among_y(source, landing, n, count, by_target):
+        def build(a, b, whole):
+            part = pl.ds(0, count if whole else L + 1)
+            return source.at[n, at_y[b], part], landing.at[n, by, part]
+
+        arrive = exchange([(0, b) for b in range(nby - 1, 0, -1)], build, by_target)
         landing[n, by, 0:count] = source[n, by, 0:count]
-        return copies
+        return arrive
 
     def wait(copies):
-        for copy in copies:
-            copy.wait_recv()
+        if callable(copies):
+            copies()
+        else:
+            for copy in copies:
+                copy.wait_recv()
 
     def spread(source, landing, n, flip, thick):
-        part = pl.ds(0, thick)
-        copies = []
-        for a, b in others:
+        def build(a, b, whole):
+            part = pl.ds(0, thick if whole else slab)
             to_x, to_y = at_x[a], at_y[b]
             if flip:
-                src, dst = source.at[n, to_x, to_y, part], landing.at[n, by, bx, part]
-            else:
-                src, dst = source.at[n, to_y, to_x, part], landing.at[n, bx, by, part]
-            copies.append(push(src, dst, {"bx": to_x, "by": to_y}))
+                return source.at[n, to_x, to_y, part], landing.at[n, by, bx, part]
+            return source.at[n, to_y, to_x, part], landing.at[n, bx, by, part]
+
+        arrive = exchange(others, build, flip)
         if flip:
             landing[n, by, bx, 0:thick] = source[n, bx, by, 0:thick]
         else:
             landing[n, bx, by, 0:thick] = source[n, by, bx, 0:thick]
-        return copies
+        return arrive
+
+    def clear_rims():
+        for n in range(2):
+            for j in range(nby):
+                a_r[n, j, L + 1:L + 3] = jnp.zeros((2, slab, C), f32)
+                for e in range(nbx):
+                    c_r[n, j, e, slab:2 * slab] = zero8
 
     def swap_groups(tiles):
         height = tiles[0].shape[0]
@@ -852,19 +903,21 @@
 
     loads[0].wait()
     charge(0, p_in, None)
+    pl.semaphore_wait(barrier, len(greeted))
+
+    def tell(at):
+        pl.semaphore_signal(
+            known.at[at], inc=1, device_id={"bx": at_x[reach[at]]}, device_id_type=MESH)
+
+    tell(0)
+    if nby == 4:
+        pl.when(jnp.logical_not(rim_slab))(clear_rims)
+    first_a = among_y(a_s, a_r, 0, L + 2, True)
     flank_start(0, p_in)
     loads[1].wait()
     relax_inside(p_in)
     charge(1, base, ring_of(0))
-    pl.semaphore_wait(barrier, len(greeted))
-
-    def tell(at):
-        pl.semaphore_signal(
-            known.at[at], inc=1, device_id={"bx": at_x[reach[at]]}, device_id_type=MESH)
-
-    tell(0)
-    first_a = among_y(a_s, a_r, 0, L + 2)
-    second_a = among_y(a_s, a_r, 1, L + 3)
+    second_a = among_y(a_s, a_r, 1, L + 3, True)
     for at in range(1, len(reach)):
         pl.semaphore_wait(known.at[at - 1], 1)
         tell(at)
@@ -917,10 +970,10 @@
     flanks = flank_send(1)
     wait(first_c)
     y_backward(0)
-    first_d = among_y(d_s, d_r, 0, L + 3)
+    first_d = among_y(d_s, d_r, 0, L + 3, False)
     wait(second_c)
     y_backward(1)
-    second_d = among_y(d_s, d_r, 1, L + 2)
+    second_d = among_y(d_s, d_r, 1, L + 2, False)
     wait(first_d)
     for l, parts in field(0):
         for c in range(3):

time: 36.8 us -> 35.6 us (0.967)
  Pallas kernels: 35.1 us -> 33.9 us
    pallas_call x1, Pallas kernels: 35.1 us -> 33.9 us  [fused_shards(): pl.pallas_call(functools.partial(fused, (L, R, C, nbx, nby)), out_shape=(...]
where the time goes in v5:
time: 35.6 us; the launch traced here: 35.5 us
  Pallas kernels  33.9 us (95%)
  other arithmetic  0.96 us (3%)
  between operations  0.64 us (2%)
    pallas_call x1, Pallas kernels, fused_shards(): pl.pallas_call(functools.partial(fused, (L, R, C, nbx, nby)), out_shape=(...  33.9 us
    neg x1, other arithmetic, fused_shards(): return (base - step_size * down, -down)  0.96 us

profile of v5, /device:TPU:0, one launch (start us, length us, event | category | flops | bytes accessed | tf_op | source)
XLA Modules:
  0.0 35.5 jit_solution(6571806053375458162)
XLA Ops:
  0.6 33.9 %shard_map.113 = (f32[3,8,32,128]{3,2,1,0:T(8,128)S(1)}, f32[3,8,32,128]{3,2,1,0:T(8,128)S(1)}) custom-call(f32[3,8,32,128]{3,2,1,0:T(8,128)} %p_h.1, f32[8,32,128]{2,1,0:T(8,128)} %alpha_h.1, f32[3,8]{1,0:T(4,128)} %landau.1, f32[8]{0:T(128)} %stiff.1, f32[8]{0:T(128)} %perm.1, f32[9]{0:T(128)} %inter.1, f32[8,256]{1,0:T(8,128)} %constant.12.clone.wx_h, ...), custom_call_target="tpu_custom_call" | custom-call | tf_op jit(solution)/shard_map/pallas_call | solution.py:1031
  34.5 1.0 %fusion = (f32[3,8,32,128]{3,2,1,0:T(8,128)}, f32[3,8,32,128]{3,2,1,0:T(8,128)}) fusion(f32[3,8,32,128]{3,2,1,0:T(8,128)S(1)} %get-tuple-element.5, f32[3,8,32,128]{3,2,1,0:T(8,128)S(1)} %get-tuple-element.4), kind=kLoop, calls=%fused_computation.1 | loop fusion | flops 294912 | bytes 1572864 | tf_op jit(solution)/shard_map/neg | solution.py:1041

commit v6 on v5

--- a/solution.py
+++ b/solution.py
@@ -502,6 +502,10 @@
     def y_prev(f, low):
         return jnp.where(lanes == 0, low, pltpu.roll(f, 1, 1))
 
+    def flush(keep):
+        while len(sends) > keep:
+            sends.pop(0)()
+
     def charge(n, src, ring):
         sides = (0, nby - 1)
         edge = zero
@@ -679,13 +683,13 @@
             s *= 2
         return tile
 
-    def y_table(full):
+    def times(full, table):
         height = full.shape[0]
         high = full.astype(jnp.bfloat16)
         wide = high.astype(f32)
         both = join([wide, full - wide], 0).astype(jnp.bfloat16)
-        first = dot(both, hy[0])
-        return first[:height] + first[height:] + dot(high, hy[1])
+        first = dot(both, hy[table, 0])
+        return first[:height] + first[height:] + dot(high, hy[table, 1])
 
     def y_forward(n):
         columns = []
@@ -709,7 +713,8 @@
                     jnp.where(lanes8 == C - 1, from_right[:, 4 * L:4 * L + 1], 0.0))
                 far = a_r[n, j, L + 2]
             columns.append(join(tiles + [near, far], 0))
-        out = y_table(join(columns, 1))
+        low, high = join(columns[:nby // 2], 1), join(columns[nby // 2:], 1)
+        out = join([times(low + high, 0), times(low - high, 1)], 1)
         tiles = [join([out[l * slab:(l + 1) * slab, t * C:(t + 1) * C] for t in range(nby)], 0)
                  for l in range(L)]
         tiles = swap_groups(tiles)
@@ -730,7 +735,9 @@
             rims.append(jnp.zeros((slab, NY), f32))
         lines = [join([tiles[l][t * slab:(t + 1) * slab] for t in range(nby)], 1)
                  for l in range(L)]
-        out = y_table(join(lines + rims, 0))
+        full = join(lines + rims, 0)
+        even, odd = times(full[:, :NY // 2], 0), times(full[:, NY // 2:], 2)
+        out = join([even + odd, even - odd], 1)
         near = out[L * slab:L * slab + L]
         for j in range(nby):
             edge = zero8
@@ -968,6 +975,7 @@
     relax_edges(flank_lines(0), col_r[0, 0], col_r[0, 1], base)
     flank_start(1, base)
     flanks = flank_send(1)
+    flush(len(flanks) + 2)
     wait(first_c)
     y_backward(0)
     first_d = among_y(d_s, d_r, 0, L + 3, False)
@@ -982,12 +990,12 @@
     rim = moved_rim()
     relax_inside(p_mid)
     relax_edges(*rim, base_o)
+    flush(1)
     wait(second_d)
     for l, parts in field(1):
         for c in range(3):
             down_o[c, l] = parts[c]
-    for send in sends:
-        send()
+    flush(0)
 
 
 def fused_shards(polarization, alpha_field, landau, stiffness, permittivity, interfaces):
@@ -998,13 +1006,16 @@
     per = C // L
     line = np.arange(grid_x)
     hx = fixed_table(line[:, None], line[None, :], grid_x)
-    line = np.arange(grid_y)
-    hy = fixed_table(line[:, None], line[None, :], grid_y)
+    line = np.arange(grid_y // 2)
+    modes = np.concatenate([2 * line, 2 * line + 1])
+    hy = jnp.stack([fixed_table(left, right, grid_y) for left, right in (
+        (line[:, None], 2 * line[None, :]), (line[:, None], 2 * line[None, :] + 1),
+        (2 * line[:, None] + 1, line[None, :]))])
     wave_x = 4.0 * np.sin(np.pi * np.arange(grid_x) / grid_x) ** 2
     wave_x = jnp.asarray(np.tile(wave_x[None, :], (8, 1)).astype(np.float32))
     at = np.arange(nbx * nby)
     first = (at % nby) * C + (at // nby) * per
-    mode = (first[:, None] + np.arange(per)[None, :]).reshape(-1)
+    mode = modes[(first[:, None] + np.arange(per)[None, :]).reshape(-1)]
     wave_y = 4.0 * np.sin(np.pi * mode / grid_y) ** 2
     wave_y = jnp.asarray(np.tile(wave_y[:, None], (1, C)).astype(np.float32))
     f32 = jnp.float32

time: 35.6 us -> 35 us (0.983)
  Pallas kernels: 33.9 us -> 33.2 us
    pallas_call x1, Pallas kernels: 33.9 us -> 33.2 us  [fused_shards(): pl.pallas_call(functools.partial(fused, (L, R, C, nbx, nby)), out_shape=(...]
where the time goes in v6:
time: 35 us; the launch traced here: 34.8 us
  Pallas kernels  33.2 us (95%)
  other arithmetic  0.96 us (3%)
  between operations  0.64 us (2%)
    pallas_call x1, Pallas kernels, fused_shards(): pl.pallas_call(functools.partial(fused, (L, R, C, nbx, nby)), out_shape=(...  33.2 us
    neg x1, other arithmetic, fused_shards(): return (base - step_size * down, -down)  0.96 us

profile of v6, /device:TPU:0, one launch (start us, length us, event | category | flops | bytes accessed | tf_op | source)
XLA Modules:
  0.0 34.8 jit_solution(7531354302290438771)
XLA Ops:
  0.6 33.2 %shard_map.131 = (f32[3,8,32,128]{3,2,1,0:T(8,128)S(1)}, f32[3,8,32,128]{3,2,1,0:T(8,128)S(1)}) custom-call(f32[3,8,32,128]{3,2,1,0:T(8,128)} %p_h.1, f32[8,32,128]{2,1,0:T(8,128)} %alpha_h.1, f32[3,8]{1,0:T(4,128)} %landau.1, f32[8]{0:T(128)} %stiff.1, f32[8]{0:T(128)} %perm.1, f32[9]{0:T(128)} %inter.1, f32[8,256]{1,0:T(8,128)} %constant.15.clone.wx_h, ...), custom_call_target="tpu_custom_call" | custom-call | tf_op jit(solution)/shard_map/pallas_call | solution.py:1042
  33.8 1.0 %fusion = (f32[3,8,32,128]{3,2,1,0:T(8,128)}, f32[3,8,32,128]{3,2,1,0:T(8,128)}) fusion(f32[3,8,32,128]{3,2,1,0:T(8,128)S(1)} %get-tuple-element.5, f32[3,8,32,128]{3,2,1,0:T(8,128)S(1)} %get-tuple-element.4), kind=kLoop, calls=%fused_computation.1 | loop fusion | flops 294912 | bytes 1572864 | tf_op jit(solution)/shard_map/neg | solution.py:1052

commit v7 on v6

--- a/solution.py
+++ b/solution.py
@@ -440,11 +440,12 @@
     return jnp.concatenate(parts, axis=axis)
 
 
-def fused(sizes, p_h, alpha_h, landau, stiff, perm, inter, wx_h, wy_h, hx_h, hy_h,
+def fused(sizes, p_h, alpha_h, landau_h, stiff_h, perm_h, inter_h, wx_h, wy_h, hx_h, hy_h,
           base_o, down_o, *scratch):
     L, R, C, nbx, nby = sizes
     (p_mid, base, coef, ratio, a_s, a_r, b_s, b_r, c_s, c_r, d_s, d_r,
-     row_s, row_r, col_s, col_r, ssem, rsem, known, p_in, alpha, wx, wy, hx, hy, local_sem) = scratch
+     row_s, row_r, col_s, col_r, ssem, rsem, known, p_in, alpha, wx, wy, hx, hy,
+     landau, stiff, perm, inter, local_sem) = scratch
     slab = R // nby
     per = C // L
     NX, NY = nbx * R, nby * C
@@ -469,7 +470,7 @@
     mine = pl.multiple_of((bx * nby + by) * per, per)
     loads = [pltpu.make_async_copy(src, dst, local_sem.at[at]) for at, (src, dst) in enumerate((
         (p_h, p_in), (alpha_h, alpha), (wx_h, wx), (wy_h.at[pl.ds(mine, per)], wy), (hx_h, hx),
-        (hy_h, hy)))]
+        (hy_h, hy), (landau_h, landau), (stiff_h, stiff), (perm_h, perm), (inter_h, inter)))]
     for load in loads:
         load.start()
 
@@ -917,11 +918,13 @@
             known.at[at], inc=1, device_id={"bx": at_x[reach[at]]}, device_id_type=MESH)
 
     tell(0)
+    first_a = among_y(a_s, a_r, 0, L + 2, True)
     if nby == 4:
         pl.when(jnp.logical_not(rim_slab))(clear_rims)
-    first_a = among_y(a_s, a_r, 0, L + 2, True)
     flank_start(0, p_in)
     loads[1].wait()
+    for load in loads[6:]:
+        load.wait()
     relax_inside(p_in)
     charge(1, base, ring_of(0))
     second_a = among_y(a_s, a_r, 1, L + 3, True)
@@ -1020,7 +1023,6 @@
     wave_y = jnp.asarray(np.tile(wave_y[:, None], (1, C)).astype(np.float32))
     f32 = jnp.float32
     hbm = pl.BlockSpec(memory_space=pltpu.HBM)
-    smem = pl.BlockSpec(memory_space=pltpu.SMEM)
     S = 2
     n_copies = S * (4 + 2 * (nby - 1) + 2 * (nbx * nby - 1))
     by_y = pltpu.VMEM((S, nby, L + 3, 8, C), f32)
@@ -1036,13 +1038,15 @@
         pltpu.SemaphoreType.REGULAR((nbx.bit_length(),)), pltpu.VMEM((3, L, R, C), f32),
         pltpu.VMEM((L, R, C), f32), pltpu.VMEM(wave_x.shape, f32), pltpu.VMEM((per, C), f32),
         pltpu.VMEM(hx.shape, hx.dtype), pltpu.VMEM(hy.shape, hy.dtype),
-        pltpu.SemaphoreType.DMA((6,)),
+        pltpu.SMEM(landau.shape, f32), pltpu.SMEM(stiffness.shape, f32),
+        pltpu.SMEM(permittivity.shape, f32), pltpu.SMEM(interfaces.shape, f32),
+        pltpu.SemaphoreType.DMA((10,)),
     ]
     out = pltpu.VMEM(polarization.shape, f32)
     base, down = pl.pallas_call(
         functools.partial(fused, (L, R, C, nbx, nby)),
         out_shape=(out, out),
-        in_specs=[hbm, hbm, smem, smem, smem, smem, hbm, hbm, hbm, hbm],
+        in_specs=[hbm] * 10,
         out_specs=(pl.BlockSpec(memory_space=pltpu.VMEM), pl.BlockSpec(memory_space=pltpu.VMEM)),
         scratch_shapes=scratch,
         compiler_params=pltpu.CompilerParams(

time: 35 us -> 34.2 us (0.977)
  Pallas kernels: 33.2 us -> 32.5 us
    pallas_call x1, Pallas kernels: 33.2 us -> 32.5 us  [fused_shards(): pl.pallas_call(functools.partial(fused, (L, R, C, nbx, nby)), out_shape=(...]
where the time goes in v7:
time: 34.2 us; the launch traced here: 34.1 us
  Pallas kernels  32.5 us (95%)
  other arithmetic  0.96 us (3%)
  between operations  0.64 us (2%)
    pallas_call x1, Pallas kernels, fused_shards(): pl.pallas_call(functools.partial(fused, (L, R, C, nbx, nby)), out_shape=(...  32.5 us
    neg x1, other arithmetic, fused_shards(): return (base - step_size * down, -down)  0.96 us

profile of v7, /device:TPU:0, one launch (start us, length us, event | category | flops | bytes accessed | tf_op | source)
XLA Modules:
  0.0 34.1 jit_solution(5739373730508353752)
XLA Ops:
  0.6 32.5 %shard_map.131 = (f32[3,8,32,128]{3,2,1,0:T(8,128)S(1)}, f32[3,8,32,128]{3,2,1,0:T(8,128)S(1)}) custom-call(f32[3,8,32,128]{3,2,1,0:T(8,128)} %p_h.1, f32[8,32,128]{2,1,0:T(8,128)} %alpha_h.1, f32[3,8]{1,0:T(4,128)} %landau_h.1, f32[8]{0:T(128)} %stiff_h.1, f32[8]{0:T(128)} %perm_h.1, f32[9]{0:T(128)} %inter_h.1, f32[8,256]{1,0:T(8,128)} %constant.15.clone.wx_h, ...), custom_call_target="tpu_custom_call" | custom-call | tf_op jit(solution)/shard_map/pallas_call | solution.py:1046
  33.1 1.0 %fusion = (f32[3,8,32,128]{3,2,1,0:T(8,128)}, f32[3,8,32,128]{3,2,1,0:T(8,128)}) fusion(f32[3,8,32,128]{3,2,1,0:T(8,128)S(1)} %get-tuple-element.5, f32[3,8,32,128]{3,2,1,0:T(8,128)S(1)} %get-tuple-element.4), kind=kLoop, calls=%fused_computation.1 | loop fusion | flops 294912 | bytes 1572864 | tf_op jit(solution)/shard_map/neg | solution.py:1056

commit v8 on v7

--- a/solution.py
+++ b/solution.py
@@ -461,7 +461,7 @@
     at_x = [partner(bx, a, nbx) for a in range(nbx)]
     at_y = [partner(by, b, nby) for b in range(nby)]
     others = [(a, b) for b in range(nby) for a in range(nbx) if a or b]
-    others.sort(key=lambda ab: -(ab[0] // 2 + ab[0] % 2 + ab[1] // 2))
+    others.sort(key=lambda ab: -(2 * (ab[0] // 4) + ab[0] // 2 % 2 + ab[0] % 2 + ab[1] // 2))
     reach = [1 << i for i in range(1, nbx.bit_length() - 1)]
     greeted = [(a, b) for a, b in others if a < 2] + [(a, 0) for a in reach]
     for a, b in greeted:

time: 34.2 us -> 34.2 us (level)
  no operation moved by 1% of the time
where the time goes in v8:
time: 34.2 us; the launch traced here: 34.1 us
  Pallas kernels  32.5 us (95%)
  other arithmetic  0.96 us (3%)
  between operations  0.64 us (2%)
    pallas_call x1, Pallas kernels, fused_shards(): pl.pallas_call(functools.partial(fused, (L, R, C, nbx, nby)), out_shape=(...  32.5 us
    neg x1, other arithmetic, fused_shards(): return (base - step_size * down, -down)  0.96 us

profile of v8, /device:TPU:0, one launch (start us, length us, event | category | flops | bytes accessed | tf_op | source)
XLA Modules:
  0.0 34.1 jit_solution(5739373730508353752)
XLA Ops:
  0.6 32.5 %shard_map.131 = (f32[3,8,32,128]{3,2,1,0:T(8,128)S(1)}, f32[3,8,32,128]{3,2,1,0:T(8,128)S(1)}) custom-call(f32[3,8,32,128]{3,2,1,0:T(8,128)} %p_h.1, f32[8,32,128]{2,1,0:T(8,128)} %alpha_h.1, f32[3,8]{1,0:T(4,128)} %landau_h.1, f32[8]{0:T(128)} %stiff_h.1, f32[8]{0:T(128)} %perm_h.1, f32[9]{0:T(128)} %inter_h.1, f32[8,256]{1,0:T(8,128)} %constant.15.clone.wx_h, ...), custom_call_target="tpu_custom_call" | custom-call | tf_op jit(solution)/shard_map/pallas_call | solution.py:1046
  33.1 1.0 %fusion = (f32[3,8,32,128]{3,2,1,0:T(8,128)}, f32[3,8,32,128]{3,2,1,0:T(8,128)}) fusion(f32[3,8,32,128]{3,2,1,0:T(8,128)S(1)} %get-tuple-element.5, f32[3,8,32,128]{3,2,1,0:T(8,128)S(1)} %get-tuple-element.4), kind=kLoop, calls=%fused_computation.1 | loop fusion | flops 294912 | bytes 1572864 | tf_op jit(solution)/shard_map/neg | solution.py:1056

commit v9 on v8

--- a/solution.py
+++ b/solution.py
@@ -997,8 +997,18 @@
     wait(second_d)
     for l, parts in field(1):
         for c in range(3):
-            down_o[c, l] = parts[c]
+            down_o[c, l] = -parts[c]
+            base_o[c, l] -= step_size * parts[c]
     flush(0)
+
+
+def hand_over(first, second, first_h, second_h, sem):
+    copies = [pltpu.make_async_copy(first, first_h, sem.at[0]),
+              pltpu.make_async_copy(second, second_h, sem.at[1])]
+    for copy in copies:
+        copy.start()
+    for copy in copies:
+        copy.wait()
 
 
 def fused_shards(polarization, alpha_field, landau, stiffness, permittivity, interfaces):
@@ -1053,7 +1063,12 @@
             collective_id=0, has_side_effects=True, vmem_limit_bytes=66 * 1000 * 1000),
     )(polarization, alpha_field, landau, stiffness, permittivity, interfaces,
       wave_x, wave_y, hx, hy)
-    return base - step_size * down, -down
+    out = jax.ShapeDtypeStruct(polarization.shape, f32)
+    chip = pl.BlockSpec(memory_space=pltpu.VMEM)
+    return pl.pallas_call(
+        hand_over, out_shape=(out, out), in_specs=[chip, chip], out_specs=(hbm, hbm),
+        scratch_shapes=[pltpu.SemaphoreType.DMA((2,))],
+    )(base, down)
 
 
 def solution(mesh):

time: 34.2 us -> 36.8 us (1.076)
  Pallas kernels: 32.5 us -> 34.5 us
  local copies, waits for them, and re-layouts: 0 us -> 1.5 us
  other arithmetic: 0.96 us -> 0 us
    pallas_call x0 -> x1, Pallas kernels: none -> 2 us  [fused_shards(): pl.pallas_call(hand_over, out_shape=(out, out), in_specs=[chip, chip], ou...]
    unnamed x0 -> x4, local copies, waits for them, and re-layouts: none -> 1.5 us
    neg x1 -> x0, other arithmetic: 0.96 us -> none  [fused_shards(): return (base - step_size * down, -down)]
where the time goes in v9:
time: 36.8 us; the launch traced here: 36.7 us
  Pallas kernels  34.5 us (94%)
  local copies, waits for them, and re-layouts  1.5 us (4%)
  between operations  0.65 us (2%)
    pallas_call x1, Pallas kernels, fused_shards(): pl.pallas_call(functools.partial(fused, (L, R, C, nbx, nby)), out_shape=(...  32.5 us
    pallas_call x1, Pallas kernels, fused_shards(): pl.pallas_call(hand_over, out_shape=(out, out), in_specs=[chip, chip], ou...  2 us
    unnamed x4, local copies, waits for them, and re-layouts  1.5 us

profile of v9, /device:TPU:0, one launch (start us, length us, event | category | flops | bytes accessed | tf_op | source)
XLA Modules:
  0.0 36.7 jit_solution(9452868234276488207)
XLA Ops:
  0.6 32.5 %shard_map.131 = (f32[3,8,32,128]{3,2,1,0:T(8,128)S(1)}, f32[3,8,32,128]{3,2,1,0:T(8,128)S(1)}) custom-call(f32[3,8,32,128]{3,2,1,0:T(8,128)} %p_h.1, f32[8,32,128]{2,1,0:T(8,128)} %alpha_h.1, f32[3,8]{1,0:T(4,128)} %landau_h.1, f32[8]{0:T(128)} %stiff_h.1, f32[8]{0:T(128)} %perm_h.1, f32[9]{0:T(128)} %inter_h.1, f32[8,256]{1,0:T(8,128)} %constant.13.clone.wx_h, ...), custom_call_target="tpu_custom_call" | custom-call | tf_op jit(solution)/shard_map/pallas_call | solution.py:1056
  33.1 0.0 copy-start
  33.2 0.7 %copy-done = f32[3,8,32,128]{3,2,1,0:T(8,128)} copy-done((f32[3,8,32,128]{3,2,1,0:T(8,128)}, f32[3,8,32,128]{3,2,1,0:T(8,128)S(1)}, u32[]{:S(2)}) %copy-start) | copy-done | bytes 393240
  33.9 0.0 copy-start.1
  33.9 0.7 %copy-done.1 = f32[3,8,32,128]{3,2,1,0:T(8,128)} copy-done((f32[3,8,32,128]{3,2,1,0:T(8,128)}, f32[3,8,32,128]{3,2,1,0:T(8,128)S(1)}, u32[]{:S(2)}) %copy-start.1) | copy-done | bytes 393240
  34.6 2.0 %shard_map.132 = (f32[3,8,32,128]{3,2,1,0:T(8,128)}, f32[3,8,32,128]{3,2,1,0:T(8,128)}) custom-call(f32[3,8,32,128]{3,2,1,0:T(8,128)} %copy-done, f32[3,8,32,128]{3,2,1,0:T(8,128)} %copy-done.1), custom_call_target="tpu_custom_call" | custom-call | tf_op jit(solution)/shard_map/pallas_call | solution.py:1068
Async XLA Ops:
  33.1 0.8 %copy-start = (f32[3,8,32,128]{3,2,1,0:T(8,128)}, f32[3,8,32,128]{3,2,1,0:T(8,128)S(1)}, u32[]{:S(2)}) copy-start(f32[3,8,32,128]{3,2,1,0:T(8,128)S(1)} %get-tuple-element.4.first) | copy-start | bytes 1179652
  33.9 0.7 %copy-start.1 = (f32[3,8,32,128]{3,2,1,0:T(8,128)}, f32[3,8,32,128]{3,2,1,0:T(8,128)S(1)}, u32[]{:S(2)}) copy-start(f32[3,8,32,128]{3,2,1,0:T(8,128)S(1)} %get-tuple-element.5.second) | copy-start | bytes 1179652
